TPU v7x, 256 devices: a whole 4x4x8 slice. The times are simulated.
256 devices in a mesh: gx: 32 (over z, y_hi, core), gy: 2 (over y_lo), gz: 4 (over x).
Axes of the slice: x: 4, y: 4 (y_hi: 2, y_lo: 2; y = y_hi * 2 + y_lo), z: 8, core: 2. Of those that a mesh axis runs over, the one named last changes fastest.
Arguments:
- displacement: float32 [3, 256, 64, 256], P(None, 'gx', 'gz', 'gy'), may hold values from -0.75 to 0.75
- velocity: float32 [3, 256, 64, 256], P(None, 'gx', 'gz', 'gy'), may hold values from -1.5 to 1.5
- classes: int32 [256, 64, 256], P('gx', 'gz', 'gy'), may hold values from 0 to 3
- clamped: int32 [256, 64, 256], P('gx', 'gz', 'gy'), may hold values 0 or 1
- stiffness: float32 [4], replicated, may hold values from 1 to 8
- softening: float32 [4], replicated, may hold values from 0.03 to 0.3
Outputs:
- final_displacement: float32 [3, 256, 64, 256], P(None, 'gx', 'gz', 'gy')
- final_velocity: float32 [3, 256, 64, 256], P(None, 'gx', 'gz', 'gy')
All inputs are finite; a program needn't handle non-finite values. No bound on the sum of `clamped` on one device may be relied on, other than what follows from the above.
Results may differ from a plain program's by a relative error of at most 0.000038.
Values sent between devices are 32-bit elements; how exact they have to be, the bound alone decides.
A program may use at most 64 MiB of HBM per device.

v0:
```python
import math

import jax
import jax.numpy as jnp
from jax import lax
from jax.sharding import PartitionSpec as P

STEPS = 4


bond_offsets = [
    (along_x, along_y, along_z)
    for along_x in range(-2, 3)
    for along_y in range(-2, 3)
    for along_z in range(-2, 3)
    if 0 < along_x * along_x + along_y * along_y + along_z * along_z <= 4
]
time_step = 0.2


def extended(x, sides, width):
    for axis, dim in sides:
        size, length = (lax.axis_size(axis), x.shape[dim])
        up = [(i, (i + 1) % size) for i in range(size - 1)]
        down = [(j, i) for i, j in up]
        last = lax.slice_in_dim(x, length - width, length, axis=dim)
        first = lax.slice_in_dim(x, 0, width, axis=dim)
        before = lax.ppermute(last, axis, up)
        after = lax.ppermute(first, axis, down)
        x = jnp.concatenate([before, x, after], axis=dim)
    return x


def bond_forces(padded, stiff_pad, soft_pad, valid_pad):
    size_x = padded.shape[1] - 4
    size_z = padded.shape[2] - 4
    size_y = padded.shape[3] - 4
    centre_part = padded[:, 2:-2, 2:-2, 2:-2]
    stiff_in = stiff_pad[2:-2, 2:-2, 2:-2]
    soft_in = soft_pad[2:-2, 2:-2, 2:-2]
    valid_in = valid_pad[2:-2, 2:-2, 2:-2]
    total_x = jnp.zeros(stiff_in.shape, jnp.float32)
    total_y = jnp.zeros(stiff_in.shape, jnp.float32)
    total_z = jnp.zeros(stiff_in.shape, jnp.float32)
    for along_x, along_y, along_z in bond_offsets:
        length = math.sqrt(along_x * along_x + along_y * along_y + along_z * along_z)
        window = (
            slice(2 + along_x, 2 + along_x + size_x),
            slice(2 + along_z, 2 + along_z + size_z),
            slice(2 + along_y, 2 + along_y + size_y),
        )
        neighbour = padded[(slice(None),) + window]
        stretch_x = neighbour[0] - centre_part[0] + along_x
        stretch_y = neighbour[1] - centre_part[1] + along_y
        stretch_z = neighbour[2] - centre_part[2] + along_z
        distance = jnp.sqrt(stretch_x * stretch_x + stretch_y * stretch_y + stretch_z * stretch_z)
        strain = (distance - length) / length
        bond_stiff = 0.5 * (stiff_in + stiff_pad[window])
        bond_soft = 0.5 * (soft_in + soft_pad[window])
        tension = (
            bond_stiff
            * strain
            * jnp.exp(-jnp.abs(strain) / bond_soft)
            * valid_pad[window]
            / (length * distance)
        )
        total_x = total_x + tension * stretch_x
        total_y = total_y + tension * stretch_y
        total_z = total_z + tension * stretch_z
    return jnp.stack([total_x, total_y, total_z]) * valid_in


def trim_rim(field_in, outer, inner):
    cut = outer - inner
    if cut == 0:
        return field_in
    return field_in[..., cut:-cut, cut:-cut, cut:-cut]


def class_lookup(class_pad, table):
    levels = jnp.arange(table.shape[0], dtype=jnp.int32)
    hits = class_pad[None, :, :, :] == levels[:, None, None, None]
    return jnp.sum(jnp.where(hits, table[:, None, None, None], 0.0), axis=0)


def inside_grid(axis_index, axis_count, count, rim_depth):
    start = axis_index * count - rim_depth
    position = start + jnp.arange(count + 2 * rim_depth, dtype=jnp.int32)
    return ((position >= 0) & (position < count * axis_count)).astype(jnp.float32)


def narrow_rim(field_in):
    return extended(field_in, (("gx", 1), ("gy", 3), ("gz", 2)), 2)


def local(displacement, velocity, classes, clamped, stiffness, softening):
    count_x, count_z, count_y = classes.shape
    rim_depth = 2
    class_pad, clamp_pad = (
        extended(classes, (("gx", 0), ("gy", 2), ("gz", 1)), rim_depth),
        extended(clamped, (("gx", 0), ("gy", 2), ("gz", 1)), rim_depth),
    )
    stiff_pad = class_lookup(class_pad, stiffness)
    soft_pad = class_lookup(class_pad, softening)
    inside_x = inside_grid(lax.axis_index("gx"), lax.axis_size("gx"), count_x, rim_depth)
    inside_z = inside_grid(lax.axis_index("gz"), lax.axis_size("gz"), count_z, rim_depth)
    inside_y = inside_grid(lax.axis_index("gy"), lax.axis_size("gy"), count_y, rim_depth)
    valid_pad = inside_x[:, None, None] * inside_z[None, :, None] * inside_y[None, None, :]
    free_pad = valid_pad * (1.0 - clamp_pad.astype(jnp.float32))
    half_step = 0.5 * time_step

    def accel_at(moved_pad, margin):
        return bond_forces(
            moved_pad,
            trim_rim(stiff_pad, rim_depth, margin),
            trim_rim(soft_pad, rim_depth, margin),
            trim_rim(valid_pad, rim_depth, margin),
        )

    free_inner = trim_rim(free_pad, rim_depth, 0)
    acceleration = accel_at(narrow_rim(displacement), 2)
    moved_field = displacement
    velocity_now = velocity
    for step_index in range(STEPS):
        half_speed = free_inner * (velocity_now + half_step * acceleration)
        moved_field = moved_field + time_step * half_speed
        acceleration = accel_at(narrow_rim(moved_field), 2)
        velocity_now = free_inner * (half_speed + half_step * acceleration)
    return (moved_field, velocity_now)


def solution(mesh):
    return jax.shard_map(
        local,
        mesh=mesh,
        in_specs=(
            P(None, "gx", "gz", "gy"),
            P(None, "gx", "gz", "gy"),
            P("gx", "gz", "gy"),
            P("gx", "gz", "gy"),
            P(),
            P(),
        ),
        out_specs=(P(None, "gx", "gz", "gy"), P(None, "gx", "gz", "gy")),
        check_vma=False,
    )
```

profile of v0, /device:TPU:121, one launch (start us, length us, event | category | flops | bytes accessed | tf_op | source)
XLA Modules:
  0.0 225.5 jit_solution(13916921383649863708)
XLA Ops:
  1.4 2.6 %collective-permute-start.7 = (s32[2,16,128]{2,1,0:T(8,128)S(1)}, s32[2,16,128]{2,1,0:T(8,128)S(1)}, u32[]{:S(2)}, u32[]{:S(2)}) collective-permute-start(s32[2,16,128]{2,1,0:T(8,128)S(1)} %get-tuple-element.303), channel_id=1, source_target_pairs={{8,0},{16,8},{24,16},{32,24},{40,32},{48,40},{56,48},{64,56},{72,6... | collective-permute-start | bytes 49160 | tf_op jit(solution)/shard_map/ppermute | solution.py:29
  4.0 6.6 %collective-permute-start.6 = (s32[2,16,128]{2,1,0:T(8,128)S(1)}, s32[2,16,128]{2,1,0:T(8,128)S(1)}, u32[]{:S(2)}, u32[]{:S(2)}) collective-permute-start(s32[2,16,128]{2,1,0:T(8,128)S(1)} %get-tuple-element.304), channel_id=1, source_target_pairs={{0,8},{8,16},{16,24},{24,32},{32,40},{40,48},{48,56},{56,64},{64,7... | collective-permute-start | bytes 49160 | tf_op jit(solution)/shard_map/ppermute | solution.py:28
  12.5 7.3 %collective-permute-start = (s32[2,16,128]{2,1,0:T(8,128)S(1)}, s32[2,16,128]{2,1,0:T(8,128)S(1)}, u32[]{:S(2)}, u32[]{:S(2)}) collective-permute-start(s32[2,16,128]{2,1,0:T(8,128)S(1)} %get-tuple-element.302), channel_id=1, source_target_pairs={{0,8},{8,16},{16,24},{24,32},{32,40},{40,48},{48,56},{56,64},{64,7... | collective-permute-start | bytes 49160 | tf_op jit(solution)/shard_map/ppermute | solution.py:28
  22.9 2.4 %collective-permute-start.13 = (f32[3,2,16,128]{3,2,1,0:T(8,128)S(1)}, f32[3,2,16,128]{3,2,1,0:T(8,128)S(1)}, u32[]{:S(2)}, u32[]{:S(2)}) collective-permute-start(f32[3,2,16,128]{3,2,1,0:T(8,128)S(1)} %get-tuple-element.296), channel_id=1, source_target_pairs={{8,0},{16,8},{24,16},{32,24},{40,32},{48,40},{56,48},{64,56},{72,6... | collective-permute-start | bytes 147464 | tf_op jit(solution)/shard_map/ppermute | solution.py:29
  26.8 4.0 %collective-permute-start.9 = (s32[12,16,2]{2,1,0:T(8,128)S(1)}, s32[12,16,2]{2,1,0:T(8,128)S(1)}, u32[]{:S(2)}, u32[]{:S(2)}) collective-permute-start(s32[12,16,2]{2,1,0:T(8,128)S(1)} %get-tuple-element.300), channel_id=1, source_target_pairs={{4,0},{5,1},{6,2},{7,3},{12,8},{13,9},{14,10},{15,11},{20,16},{21,... | collective-permute-start | bytes 4616 | tf_op jit(solution)/shard_map/ppermute | solution.py:29
  33.7 3.1 %collective-permute-start.10 = (s32[12,2,132]{2,1,0:T(2,128)S(1)}, s32[12,2,132]{2,1,0:T(2,128)S(1)}, u32[]{:S(2)}, u32[]{:S(2)}) collective-permute-start(s32[12,2,132]{2,1,0:T(2,128)S(1)} %get-tuple-element.282), channel_id=1, source_target_pairs={{0,1},{1,2},{2,3},{4,5},{5,6},{6,7},{8,9},{9,10},{10,11},{12,13},{... | collective-permute-start | bytes 38024 | tf_op jit(solution)/shard_map/ppermute | solution.py:28
  38.3 4.0 %collective-permute-start.4 = (s32[12,2,132]{2,1,0:T(2,128)S(1)}, s32[12,2,132]{2,1,0:T(2,128)S(1)}, u32[]{:S(2)}, u32[]{:S(2)}) collective-permute-start(s32[12,2,132]{2,1,0:T(2,128)S(1)} %get-tuple-element.243), channel_id=1, source_target_pairs={{0,1},{1,2},{2,3},{4,5},{5,6},{6,7},{8,9},{9,10},{10,11},{12,13},{... | collective-permute-start | bytes 38024 | tf_op jit(solution)/shard_map/ppermute | solution.py:28
  48.5 4.0 %collective-permute-start.15 = (f32[3,12,16,2]{3,2,1,0:T(8,128)S(1)}, f32[3,12,16,2]{3,2,1,0:T(8,128)S(1)}, u32[]{:S(2)}, u32[]{:S(2)}) collective-permute-start(f32[3,12,16,2]{3,2,1,0:T(8,128)S(1)} %get-tuple-element.281), channel_id=1, source_target_pairs={{4,0},{5,1},{6,2},{7,3},{12,8},{13,9},{14,10},{15,11},{20,16},{21,... | collective-permute-start | bytes 13832 | tf_op jit(solution)/shard_map/ppermute | solution.py:29
  52.7 3.0 %collective-permute-done.14 = f32[3,12,16,2]{3,2,1,0:T(8,128)S(1)} collective-permute-done((f32[3,12,16,2]{3,2,1,0:T(8,128)S(1)}, f32[3,12,16,2]{3,2,1,0:T(8,128)S(1)}, u32[]{:S(2)}, u32[]{:S(2)}) %collective-permute-start.14) | collective-permute-done | bytes 4640 | tf_op jit(solution)/shard_map/ppermute | solution.py:28
  58.2 4.3 %collective-permute-start.16 = (f32[3,12,2,132]{3,2,1,0:T(2,128)S(1)}, f32[3,12,2,132]{3,2,1,0:T(2,128)S(1)}, u32[]{:S(2)}, u32[]{:S(2)}) collective-permute-start(f32[3,12,2,132]{3,2,1,0:T(2,128)S(1)} %get-tuple-element.222), channel_id=1, source_target_pairs={{0,1},{1,2},{2,3},{4,5},{5,6},{6,7},{8,9},{9,10},{10,11},{12,13},{... | collective-permute-start | bytes 114056 | tf_op jit(solution)/shard_map/ppermute | solution.py:28
  64.6 4.9 %add_bitcast_fusion.14 = (f32[1,8,16,128]{3,2,1,0:T(8,128)S(1)}, f32[8,16,128]{2,1,0:T(8,128)S(1)}, f32[8,16,128]{2,1,0:T(8,128)S(1)}, f32[8,16,128]{2,1,0:T(8,1...) fusion(f32[8,16,128]{2,1,0:T(8,128)S(1)} %get-tuple-element.200, ...), kind=kLoop, calls=%fused_computation.1806 | loop fusion | flops 12484608 | bytes 15311872 | tf_op jit(solution)/shard_map/stack | solution.py:70
  71.2 10.2 %collective-permute-start.18 = (f32[3,2,16,128]{3,2,1,0:T(8,128)S(1)}, f32[3,2,16,128]{3,2,1,0:T(8,128)S(1)}, u32[]{:S(2)}, u32[]{:S(2)}) collective-permute-start(f32[3,2,16,128]{3,2,1,0:T(8,128)S(1)} %get-tuple-element.290), channel_id=1, source_target_pairs={{0,8},{8,16},{16,24},{24,32},{32,40},{40,48},{48,56},{56,64},{64,7... | collective-permute-start | bytes 147464 | tf_op jit(solution)/shard_map/ppermute | solution.py:28
  83.3 7.1 %collective-permute-done.19 = f32[3,2,16,128]{3,2,1,0:T(8,128)S(1)} collective-permute-done((f32[3,2,16,128]{3,2,1,0:T(8,128)S(1)}, f32[3,2,16,128]{3,2,1,0:T(8,128)S(1)}, u32[]{:S(2)}, u32[]{:S(2)}) %collective-permute-start.19) | collective-permute-done | bytes 49184 | tf_op jit(solution)/shard_map/ppermute | solution.py:29
  90.6 3.5 %collective-permute-start.21 = (f32[3,12,16,2]{3,2,1,0:T(8,128)S(1)}, f32[3,12,16,2]{3,2,1,0:T(8,128)S(1)}, u32[]{:S(2)}, u32[]{:S(2)}) collective-permute-start(f32[3,12,16,2]{3,2,1,0:T(8,128)S(1)} %get-tuple-element.239), channel_id=1, source_target_pairs={{4,0},{5,1},{6,2},{7,3},{12,8},{13,9},{14,10},{15,11},{20,16},{21,... | collective-permute-start | bytes 13832 | tf_op jit(solution)/shard_map/ppermute | solution.py:29
  97.8 3.8 %collective-permute-done.20 = f32[3,12,16,2]{3,2,1,0:T(8,128)S(1)} collective-permute-done((f32[3,12,16,2]{3,2,1,0:T(8,128)S(1)}, f32[3,12,16,2]{3,2,1,0:T(8,128)S(1)}, u32[]{:S(2)}, u32[]{:S(2)}) %collective-permute-start.20) | collective-permute-done | bytes 4640 | tf_op jit(solution)/shard_map/ppermute | solution.py:28
  103.2 4.6 %collective-permute-start.22 = (f32[3,12,2,132]{3,2,1,0:T(2,128)S(1)}, f32[3,12,2,132]{3,2,1,0:T(2,128)S(1)}, u32[]{:S(2)}, u32[]{:S(2)}) collective-permute-start(f32[3,12,2,132]{3,2,1,0:T(2,128)S(1)} %get-tuple-element.218), channel_id=1, source_target_pairs={{0,1},{1,2},{2,3},{4,5},{5,6},{6,7},{8,9},{9,10},{10,11},{12,13},{... | collective-permute-start | bytes 114056 | tf_op jit(solution)/shard_map/ppermute | solution.py:28
  109.9 4.5 %add_bitcast_fusion.11 = (f32[1,8,16,128]{3,2,1,0:T(8,128)S(1)}, f32[8,16,128]{2,1,0:T(8,128)S(1)}, f32[8,16,128]{2,1,0:T(8,128)S(1)}, f32[8,16,128]{2,1,0:T(8,1...) fusion(f32[3,12,16,130]{3,2,1,0:T(8,128)S(1)} %get-tuple-elemen, ...), kind=kLoop, calls=%fused_computation.1771 | loop fusion | flops 11616256 | bytes 14581760 | tf_op jit(solution)/shard_map/stack | solution.py:70
  115.6 5.0 %collective-permute-start.24 = (f32[3,2,16,128]{3,2,1,0:T(8,128)S(1)}, f32[3,2,16,128]{3,2,1,0:T(8,128)S(1)}, u32[]{:S(2)}, u32[]{:S(2)}) collective-permute-start(f32[3,2,16,128]{3,2,1,0:T(8,128)S(1)} %get-tuple-element.288), channel_id=1, source_target_pairs={{0,8},{8,16},{16,24},{24,32},{32,40},{40,48},{48,56},{56,64},{64,7... | collective-permute-start | bytes 147464 | tf_op jit(solution)/shard_map/ppermute | solution.py:28
  122.5 7.2 %collective-permute-done.25 = f32[3,2,16,128]{3,2,1,0:T(8,128)S(1)} collective-permute-done((f32[3,2,16,128]{3,2,1,0:T(8,128)S(1)}, f32[3,2,16,128]{3,2,1,0:T(8,128)S(1)}, u32[]{:S(2)}, u32[]{:S(2)}) %collective-permute-start.25) | collective-permute-done | bytes 49184 | tf_op jit(solution)/shard_map/ppermute | solution.py:29
  134.8 3.8 %collective-permute-done.26 = f32[3,12,16,2]{3,2,1,0:T(8,128)S(1)} collective-permute-done((f32[3,12,16,2]{3,2,1,0:T(8,128)S(1)}, f32[3,12,16,2]{3,2,1,0:T(8,128)S(1)}, u32[]{:S(2)}, u32[]{:S(2)}) %collective-permute-start.26) | collective-permute-done | bytes 4640 | tf_op jit(solution)/shard_map/ppermute | solution.py:28
  140.3 4.8 %collective-permute-start.28 = (f32[3,12,2,132]{3,2,1,0:T(2,128)S(1)}, f32[3,12,2,132]{3,2,1,0:T(2,128)S(1)}, u32[]{:S(2)}, u32[]{:S(2)}) collective-permute-start(f32[3,12,2,132]{3,2,1,0:T(2,128)S(1)} %get-tuple-element.214), channel_id=1, source_target_pairs={{0,1},{1,2},{2,3},{4,5},{5,6},{6,7},{8,9},{9,10},{10,11},{12,13},{... | collective-permute-start | bytes 114056 | tf_op jit(solution)/shard_map/ppermute | solution.py:28
  146.9 4.5 %add_bitcast_fusion.8 = (f32[1,8,16,128]{3,2,1,0:T(8,128)S(1)}, f32[8,16,128]{2,1,0:T(8,128)S(1)}, f32[8,16,128]{2,1,0:T(8,128)S(1)}, f32[8,16,128]{2,1,0:T(8,12...) fusion(f32[3,12,16,130]{3,2,1,0:T(8,128)S(1)} %get-tuple-elemen, ...), kind=kLoop, calls=%fused_computation.1736 | loop fusion | flops 11616256 | bytes 14581760 | tf_op jit(solution)/shard_map/stack | solution.py:70
  152.7 3.9 %collective-permute-start.30 = (f32[3,2,16,128]{3,2,1,0:T(8,128)S(1)}, f32[3,2,16,128]{3,2,1,0:T(8,128)S(1)}, u32[]{:S(2)}, u32[]{:S(2)}) collective-permute-start(f32[3,2,16,128]{3,2,1,0:T(8,128)S(1)} %get-tuple-element.286), channel_id=1, source_target_pairs={{0,8},{8,16},{16,24},{24,32},{32,40},{40,48},{48,56},{56,64},{64,7... | collective-permute-start | bytes 147464 | tf_op jit(solution)/shard_map/ppermute | solution.py:28
  158.6 7.2 %collective-permute-done.31 = f32[3,2,16,128]{3,2,1,0:T(8,128)S(1)} collective-permute-done((f32[3,2,16,128]{3,2,1,0:T(8,128)S(1)}, f32[3,2,16,128]{3,2,1,0:T(8,128)S(1)}, u32[]{:S(2)}, u32[]{:S(2)}) %collective-permute-start.31) | collective-permute-done | bytes 49184 | tf_op jit(solution)/shard_map/ppermute | solution.py:29
  170.9 3.8 %collective-permute-done.32 = f32[3,12,16,2]{3,2,1,0:T(8,128)S(1)} collective-permute-done((f32[3,12,16,2]{3,2,1,0:T(8,128)S(1)}, f32[3,12,16,2]{3,2,1,0:T(8,128)S(1)}, u32[]{:S(2)}, u32[]{:S(2)}) %collective-permute-start.32) | collective-permute-done | bytes 4640 | tf_op jit(solution)/shard_map/ppermute | solution.py:28
  176.3 4.6 %collective-permute-start.34 = (f32[3,12,2,132]{3,2,1,0:T(2,128)S(1)}, f32[3,12,2,132]{3,2,1,0:T(2,128)S(1)}, u32[]{:S(2)}, u32[]{:S(2)}) collective-permute-start(f32[3,12,2,132]{3,2,1,0:T(2,128)S(1)} %get-tuple-element.210), channel_id=1, source_target_pairs={{0,1},{1,2},{2,3},{4,5},{5,6},{6,7},{8,9},{9,10},{10,11},{12,13},{... | collective-permute-start | bytes 114056 | tf_op jit(solution)/shard_map/ppermute | solution.py:28
  183.0 4.5 %add_bitcast_fusion.5 = (f32[1,8,16,128]{3,2,1,0:T(8,128)S(1)}, f32[8,16,128]{2,1,0:T(8,128)S(1)}, f32[8,16,128]{2,1,0:T(8,128)S(1)}, f32[8,16,128]{2,1,0:T(8,12...) fusion(f32[3,12,16,130]{3,2,1,0:T(8,128)S(1)} %get-tuple-elemen, ...), kind=kLoop, calls=%fused_computation.1701 | loop fusion | flops 11616256 | bytes 14581760 | tf_op jit(solution)/shard_map/stack | solution.py:70
  188.7 3.9 %collective-permute-start.36 = (f32[3,2,16,128]{3,2,1,0:T(8,128)S(1)}, f32[3,2,16,128]{3,2,1,0:T(8,128)S(1)}, u32[]{:S(2)}, u32[]{:S(2)}) collective-permute-start(f32[3,2,16,128]{3,2,1,0:T(8,128)S(1)} %get-tuple-element.284), channel_id=1, source_target_pairs={{0,8},{8,16},{16,24},{24,32},{32,40},{40,48},{48,56},{56,64},{64,7... | collective-permute-start | bytes 147464 | tf_op jit(solution)/shard_map/ppermute | solution.py:28
  194.6 7.2 %collective-permute-done.37 = f32[3,2,16,128]{3,2,1,0:T(8,128)S(1)} collective-permute-done((f32[3,2,16,128]{3,2,1,0:T(8,128)S(1)}, f32[3,2,16,128]{3,2,1,0:T(8,128)S(1)}, u32[]{:S(2)}, u32[]{:S(2)}) %collective-permute-start.37) | collective-permute-done | bytes 49184 | tf_op jit(solution)/shard_map/ppermute | solution.py:29
  206.9 3.8 %collective-permute-done.38 = f32[3,12,16,2]{3,2,1,0:T(8,128)S(1)} collective-permute-done((f32[3,12,16,2]{3,2,1,0:T(8,128)S(1)}, f32[3,12,16,2]{3,2,1,0:T(8,128)S(1)}, u32[]{:S(2)}, u32[]{:S(2)}) %collective-permute-start.38) | collective-permute-done | bytes 4640 | tf_op jit(solution)/shard_map/ppermute | solution.py:28
  212.4 4.6 %collective-permute-start.40 = (f32[3,12,2,132]{3,2,1,0:T(2,128)S(1)}, f32[3,12,2,132]{3,2,1,0:T(2,128)S(1)}, u32[]{:S(2)}, u32[]{:S(2)}) collective-permute-start(f32[3,12,2,132]{3,2,1,0:T(2,128)S(1)} %get-tuple-element.206), channel_id=1, source_target_pairs={{0,1},{1,2},{2,3},{4,5},{5,6},{6,7},{8,9},{9,10},{10,11},{12,13},{... | collective-permute-start | bytes 114056 | tf_op jit(solution)/shard_map/ppermute | solution.py:28
  219.0 4.5 %add_bitcast_fusion.2 = (f32[1,8,16,128]{3,2,1,0:T(8,128)S(1)}, f32[8,16,128]{2,1,0:T(8,128)S(1)}, f32[8,16,128]{2,1,0:T(8,128)S(1)}, f32[8,16,128]{2,1,0:T(8,12...) fusion(f32[3,12,16,130]{3,2,1,0:T(8,128)S(1)} %get-tuple-elemen, ...), kind=kLoop, calls=%fused_computation.1666 | loop fusion | flops 11616256 | bytes 14581760 | tf_op jit(solution)/shard_map/stack | solution.py:70
  (147 shorter events, 70.3 us)
Async XLA Ops:
  1.4 23.9 %collective-permute-start.7 = (s32[2,16,128]{2,1,0:T(8,128)S(1)}, s32[2,16,128]{2,1,0:T(8,128)S(1)}, u32[]{:S(2)}, u32[]{:S(2)}) collective-permute-start(s32[2,16,128]{2,1,0:T(8,128)S(1)} %get-tuple-element.303), channel_id=1, source_target_pairs={{8,0},{16,8},{24,16},{32,24},{40,32},{48,40},{56,48},{64,56},{72,6... | collective-permute-start | bytes 49160 | tf_op jit(solution)/shard_map/ppermute | solution.py:29
  4.0 18.9 %collective-permute-start.6 = (s32[2,16,128]{2,1,0:T(8,128)S(1)}, s32[2,16,128]{2,1,0:T(8,128)S(1)}, u32[]{:S(2)}, u32[]{:S(2)}) collective-permute-start(s32[2,16,128]{2,1,0:T(8,128)S(1)} %get-tuple-element.304), channel_id=1, source_target_pairs={{0,8},{8,16},{16,24},{24,32},{32,40},{40,48},{48,56},{56,64},{64,7... | collective-permute-start | bytes 49160 | tf_op jit(solution)/shard_map/ppermute | solution.py:28
  10.6 20.2 %collective-permute-start.1 = (s32[2,16,128]{2,1,0:T(8,128)S(1)}, s32[2,16,128]{2,1,0:T(8,128)S(1)}, u32[]{:S(2)}, u32[]{:S(2)}) collective-permute-start(s32[2,16,128]{2,1,0:T(8,128)S(1)} %get-tuple-element.301), channel_id=1, source_target_pairs={{8,0},{16,8},{24,16},{32,24},{40,32},{48,40},{56,48},{64,56},{72,6... | collective-permute-start | bytes 49160 | tf_op jit(solution)/shard_map/ppermute | solution.py:29
  12.5 12.9 %collective-permute-start = (s32[2,16,128]{2,1,0:T(8,128)S(1)}, s32[2,16,128]{2,1,0:T(8,128)S(1)}, u32[]{:S(2)}, u32[]{:S(2)}) collective-permute-start(s32[2,16,128]{2,1,0:T(8,128)S(1)} %get-tuple-element.302), channel_id=1, source_target_pairs={{0,8},{8,16},{16,24},{24,32},{32,40},{40,48},{48,56},{56,64},{64,7... | collective-permute-start | bytes 49160 | tf_op jit(solution)/shard_map/ppermute | solution.py:28
  20.6 25.6 %collective-permute-start.12 = (f32[3,2,16,128]{3,2,1,0:T(8,128)S(1)}, f32[3,2,16,128]{3,2,1,0:T(8,128)S(1)}, u32[]{:S(2)}, u32[]{:S(2)}) collective-permute-start(f32[3,2,16,128]{3,2,1,0:T(8,128)S(1)} %get-tuple-element.295), channel_id=1, source_target_pairs={{0,8},{8,16},{16,24},{24,32},{32,40},{40,48},{48,56},{56,64},{64,7... | collective-permute-start | bytes 147464 | tf_op jit(solution)/shard_map/ppermute | solution.py:28
  22.9 24.1 %collective-permute-start.13 = (f32[3,2,16,128]{3,2,1,0:T(8,128)S(1)}, f32[3,2,16,128]{3,2,1,0:T(8,128)S(1)}, u32[]{:S(2)}, u32[]{:S(2)}) collective-permute-start(f32[3,2,16,128]{3,2,1,0:T(8,128)S(1)} %get-tuple-element.296), channel_id=1, source_target_pairs={{8,0},{16,8},{24,16},{32,24},{40,32},{48,40},{56,48},{64,56},{72,6... | collective-permute-start | bytes 147464 | tf_op jit(solution)/shard_map/ppermute | solution.py:29
  25.5 6.7 %collective-permute-start.8 = (s32[12,16,2]{2,1,0:T(8,128)S(1)}, s32[12,16,2]{2,1,0:T(8,128)S(1)}, u32[]{:S(2)}, u32[]{:S(2)}) collective-permute-start(s32[12,16,2]{2,1,0:T(8,128)S(1)} %get-tuple-element.299), channel_id=1, source_target_pairs={{0,4},{1,5},{2,6},{3,7},{8,12},{9,13},{10,14},{11,15},{16,20},{17,... | collective-permute-start | bytes 4616 | tf_op jit(solution)/shard_map/ppermute | solution.py:28
  26.8 6.7 %collective-permute-start.9 = (s32[12,16,2]{2,1,0:T(8,128)S(1)}, s32[12,16,2]{2,1,0:T(8,128)S(1)}, u32[]{:S(2)}, u32[]{:S(2)}) collective-permute-start(s32[12,16,2]{2,1,0:T(8,128)S(1)} %get-tuple-element.300), channel_id=1, source_target_pairs={{4,0},{5,1},{6,2},{7,3},{12,8},{13,9},{14,10},{15,11},{20,16},{21,... | collective-permute-start | bytes 4616 | tf_op jit(solution)/shard_map/ppermute | solution.py:29
  33.7 8.6 %collective-permute-start.10 = (s32[12,2,132]{2,1,0:T(2,128)S(1)}, s32[12,2,132]{2,1,0:T(2,128)S(1)}, u32[]{:S(2)}, u32[]{:S(2)}) collective-permute-start(s32[12,2,132]{2,1,0:T(2,128)S(1)} %get-tuple-element.282), channel_id=1, source_target_pairs={{0,1},{1,2},{2,3},{4,5},{5,6},{6,7},{8,9},{9,10},{10,11},{12,13},{... | collective-permute-start | bytes 38024 | tf_op jit(solution)/shard_map/ppermute | solution.py:28
  36.8 6.8 %collective-permute-start.11 = (s32[12,2,132]{2,1,0:T(2,128)S(1)}, s32[12,2,132]{2,1,0:T(2,128)S(1)}, u32[]{:S(2)}, u32[]{:S(2)}) collective-permute-start(s32[12,2,132]{2,1,0:T(2,128)S(1)} %get-tuple-element.283), channel_id=1, source_target_pairs={{1,0},{2,1},{3,2},{5,4},{6,5},{7,6},{9,8},{10,9},{11,10},{13,12},{... | collective-permute-start | bytes 38024 | tf_op jit(solution)/shard_map/ppermute | solution.py:29
  38.3 14.2 %collective-permute-start.4 = (s32[12,2,132]{2,1,0:T(2,128)S(1)}, s32[12,2,132]{2,1,0:T(2,128)S(1)}, u32[]{:S(2)}, u32[]{:S(2)}) collective-permute-start(s32[12,2,132]{2,1,0:T(2,128)S(1)} %get-tuple-element.243), channel_id=1, source_target_pairs={{0,1},{1,2},{2,3},{4,5},{5,6},{6,7},{8,9},{9,10},{10,11},{12,13},{... | collective-permute-start | bytes 38024 | tf_op jit(solution)/shard_map/ppermute | solution.py:28
  42.3 10.2 %collective-permute-start.5 = (s32[12,2,132]{2,1,0:T(2,128)S(1)}, s32[12,2,132]{2,1,0:T(2,128)S(1)}, u32[]{:S(2)}, u32[]{:S(2)}) collective-permute-start(s32[12,2,132]{2,1,0:T(2,128)S(1)} %get-tuple-element.244), channel_id=1, source_target_pairs={{1,0},{2,1},{3,2},{5,4},{6,5},{7,6},{9,8},{10,9},{11,10},{13,12},{... | collective-permute-start | bytes 38024 | tf_op jit(solution)/shard_map/ppermute | solution.py:29
  47.2 8.6 %collective-permute-start.14 = (f32[3,12,16,2]{3,2,1,0:T(8,128)S(1)}, f32[3,12,16,2]{3,2,1,0:T(8,128)S(1)}, u32[]{:S(2)}, u32[]{:S(2)}) collective-permute-start(f32[3,12,16,2]{3,2,1,0:T(8,128)S(1)} %get-tuple-element.280), channel_id=1, source_target_pairs={{0,4},{1,5},{2,6},{3,7},{8,12},{9,13},{10,14},{11,15},{16,20},{17,... | collective-permute-start | bytes 13832 | tf_op jit(solution)/shard_map/ppermute | solution.py:28
  48.5 8.2 %collective-permute-start.15 = (f32[3,12,16,2]{3,2,1,0:T(8,128)S(1)}, f32[3,12,16,2]{3,2,1,0:T(8,128)S(1)}, u32[]{:S(2)}, u32[]{:S(2)}) collective-permute-start(f32[3,12,16,2]{3,2,1,0:T(8,128)S(1)} %get-tuple-element.281), channel_id=1, source_target_pairs={{4,0},{5,1},{6,2},{7,3},{12,8},{13,9},{14,10},{15,11},{20,16},{21,... | collective-permute-start | bytes 13832 | tf_op jit(solution)/shard_map/ppermute | solution.py:29
  71.2 12.1 %collective-permute-start.18 = (f32[3,2,16,128]{3,2,1,0:T(8,128)S(1)}, f32[3,2,16,128]{3,2,1,0:T(8,128)S(1)}, u32[]{:S(2)}, u32[]{:S(2)}) collective-permute-start(f32[3,2,16,128]{3,2,1,0:T(8,128)S(1)} %get-tuple-element.290), channel_id=1, source_target_pairs={{0,8},{8,16},{16,24},{24,32},{32,40},{40,48},{48,56},{56,64},{64,7... | collective-permute-start | bytes 147464 | tf_op jit(solution)/shard_map/ppermute | solution.py:28
  81.4 9.1 %collective-permute-start.19 = (f32[3,2,16,128]{3,2,1,0:T(8,128)S(1)}, f32[3,2,16,128]{3,2,1,0:T(8,128)S(1)}, u32[]{:S(2)}, u32[]{:S(2)}) collective-permute-start(f32[3,2,16,128]{3,2,1,0:T(8,128)S(1)} %get-tuple-element.291), channel_id=1, source_target_pairs={{8,0},{16,8},{24,16},{32,24},{40,32},{48,40},{56,48},{64,56},{72,6... | collective-permute-start | bytes 147464 | tf_op jit(solution)/shard_map/ppermute | solution.py:29
  90.6 7.1 %collective-permute-start.21 = (f32[3,12,16,2]{3,2,1,0:T(8,128)S(1)}, f32[3,12,16,2]{3,2,1,0:T(8,128)S(1)}, u32[]{:S(2)}, u32[]{:S(2)}) collective-permute-start(f32[3,12,16,2]{3,2,1,0:T(8,128)S(1)} %get-tuple-element.239), channel_id=1, source_target_pairs={{4,0},{5,1},{6,2},{7,3},{12,8},{13,9},{14,10},{15,11},{20,16},{21,... | collective-permute-start | bytes 13832 | tf_op jit(solution)/shard_map/ppermute | solution.py:29
  94.1 7.5 %collective-permute-start.20 = (f32[3,12,16,2]{3,2,1,0:T(8,128)S(1)}, f32[3,12,16,2]{3,2,1,0:T(8,128)S(1)}, u32[]{:S(2)}, u32[]{:S(2)}) collective-permute-start(f32[3,12,16,2]{3,2,1,0:T(8,128)S(1)} %get-tuple-element.240), channel_id=1, source_target_pairs={{0,4},{1,5},{2,6},{3,7},{8,12},{9,13},{10,14},{11,15},{16,20},{17,... | collective-permute-start | bytes 13832 | tf_op jit(solution)/shard_map/ppermute | solution.py:28
  101.9 6.2 %collective-permute-start.23 = (f32[3,12,2,132]{3,2,1,0:T(2,128)S(1)}, f32[3,12,2,132]{3,2,1,0:T(2,128)S(1)}, u32[]{:S(2)}, u32[]{:S(2)}) collective-permute-start(f32[3,12,2,132]{3,2,1,0:T(2,128)S(1)} %get-tuple-element.217), channel_id=1, source_target_pairs={{1,0},{2,1},{3,2},{5,4},{6,5},{7,6},{9,8},{10,9},{11,10},{13,12},{... | collective-permute-start | bytes 114056 | tf_op jit(solution)/shard_map/ppermute | solution.py:29
  103.2 6.0 %collective-permute-start.22 = (f32[3,12,2,132]{3,2,1,0:T(2,128)S(1)}, f32[3,12,2,132]{3,2,1,0:T(2,128)S(1)}, u32[]{:S(2)}, u32[]{:S(2)}) collective-permute-start(f32[3,12,2,132]{3,2,1,0:T(2,128)S(1)} %get-tuple-element.218), channel_id=1, source_target_pairs={{0,1},{1,2},{2,3},{4,5},{5,6},{6,7},{8,9},{9,10},{10,11},{12,13},{... | collective-permute-start | bytes 114056 | tf_op jit(solution)/shard_map/ppermute | solution.py:28
  115.6 6.9 %collective-permute-start.24 = (f32[3,2,16,128]{3,2,1,0:T(8,128)S(1)}, f32[3,2,16,128]{3,2,1,0:T(8,128)S(1)}, u32[]{:S(2)}, u32[]{:S(2)}) collective-permute-start(f32[3,2,16,128]{3,2,1,0:T(8,128)S(1)} %get-tuple-element.288), channel_id=1, source_target_pairs={{0,8},{8,16},{16,24},{24,32},{32,40},{40,48},{48,56},{56,64},{64,7... | collective-permute-start | bytes 147464 | tf_op jit(solution)/shard_map/ppermute | solution.py:28
  120.6 9.1 %collective-permute-start.25 = (f32[3,2,16,128]{3,2,1,0:T(8,128)S(1)}, f32[3,2,16,128]{3,2,1,0:T(8,128)S(1)}, u32[]{:S(2)}, u32[]{:S(2)}) collective-permute-start(f32[3,2,16,128]{3,2,1,0:T(8,128)S(1)} %get-tuple-element.289), channel_id=1, source_target_pairs={{8,0},{16,8},{24,16},{32,24},{40,32},{48,40},{56,48},{64,56},{72,6... | collective-permute-start | bytes 147464 | tf_op jit(solution)/shard_map/ppermute | solution.py:29
  131.2 7.5 %collective-permute-start.26 = (f32[3,12,16,2]{3,2,1,0:T(8,128)S(1)}, f32[3,12,16,2]{3,2,1,0:T(8,128)S(1)}, u32[]{:S(2)}, u32[]{:S(2)}) collective-permute-start(f32[3,12,16,2]{3,2,1,0:T(8,128)S(1)} %get-tuple-element.236), channel_id=1, source_target_pairs={{0,4},{1,5},{2,6},{3,7},{8,12},{9,13},{10,14},{11,15},{16,20},{17,... | collective-permute-start | bytes 13832 | tf_op jit(solution)/shard_map/ppermute | solution.py:28
  139.0 6.4 %collective-permute-start.29 = (f32[3,12,2,132]{3,2,1,0:T(2,128)S(1)}, f32[3,12,2,132]{3,2,1,0:T(2,128)S(1)}, u32[]{:S(2)}, u32[]{:S(2)}) collective-permute-start(f32[3,12,2,132]{3,2,1,0:T(2,128)S(1)} %get-tuple-element.213), channel_id=1, source_target_pairs={{1,0},{2,1},{3,2},{5,4},{6,5},{7,6},{9,8},{10,9},{11,10},{13,12},{... | collective-permute-start | bytes 114056 | tf_op jit(solution)/shard_map/ppermute | solution.py:29
  140.3 6.0 %collective-permute-start.28 = (f32[3,12,2,132]{3,2,1,0:T(2,128)S(1)}, f32[3,12,2,132]{3,2,1,0:T(2,128)S(1)}, u32[]{:S(2)}, u32[]{:S(2)}) collective-permute-start(f32[3,12,2,132]{3,2,1,0:T(2,128)S(1)} %get-tuple-element.214), channel_id=1, source_target_pairs={{0,1},{1,2},{2,3},{4,5},{5,6},{6,7},{8,9},{9,10},{10,11},{12,13},{... | collective-permute-start | bytes 114056 | tf_op jit(solution)/shard_map/ppermute | solution.py:28
  156.6 9.1 %collective-permute-start.31 = (f32[3,2,16,128]{3,2,1,0:T(8,128)S(1)}, f32[3,2,16,128]{3,2,1,0:T(8,128)S(1)}, u32[]{:S(2)}, u32[]{:S(2)}) collective-permute-start(f32[3,2,16,128]{3,2,1,0:T(8,128)S(1)} %get-tuple-element.287), channel_id=1, source_target_pairs={{8,0},{16,8},{24,16},{32,24},{40,32},{48,40},{56,48},{64,56},{72,6... | collective-permute-start | bytes 147464 | tf_op jit(solution)/shard_map/ppermute | solution.py:29
  167.2 7.5 %collective-permute-start.32 = (f32[3,12,16,2]{3,2,1,0:T(8,128)S(1)}, f32[3,12,16,2]{3,2,1,0:T(8,128)S(1)}, u32[]{:S(2)}, u32[]{:S(2)}) collective-permute-start(f32[3,12,16,2]{3,2,1,0:T(8,128)S(1)} %get-tuple-element.232), channel_id=1, source_target_pairs={{0,4},{1,5},{2,6},{3,7},{8,12},{9,13},{10,14},{11,15},{16,20},{17,... | collective-permute-start | bytes 13832 | tf_op jit(solution)/shard_map/ppermute | solution.py:28
  175.0 6.2 %collective-permute-start.35 = (f32[3,12,2,132]{3,2,1,0:T(2,128)S(1)}, f32[3,12,2,132]{3,2,1,0:T(2,128)S(1)}, u32[]{:S(2)}, u32[]{:S(2)}) collective-permute-start(f32[3,12,2,132]{3,2,1,0:T(2,128)S(1)} %get-tuple-element.209), channel_id=1, source_target_pairs={{1,0},{2,1},{3,2},{5,4},{6,5},{7,6},{9,8},{10,9},{11,10},{13,12},{... | collective-permute-start | bytes 114056 | tf_op jit(solution)/shard_map/ppermute | solution.py:29
  192.7 9.1 %collective-permute-start.37 = (f32[3,2,16,128]{3,2,1,0:T(8,128)S(1)}, f32[3,2,16,128]{3,2,1,0:T(8,128)S(1)}, u32[]{:S(2)}, u32[]{:S(2)}) collective-permute-start(f32[3,2,16,128]{3,2,1,0:T(8,128)S(1)} %get-tuple-element.285), channel_id=1, source_target_pairs={{8,0},{16,8},{24,16},{32,24},{40,32},{48,40},{56,48},{64,56},{72,6... | collective-permute-start | bytes 147464 | tf_op jit(solution)/shard_map/ppermute | solution.py:29
  203.3 7.5 %collective-permute-start.38 = (f32[3,12,16,2]{3,2,1,0:T(8,128)S(1)}, f32[3,12,16,2]{3,2,1,0:T(8,128)S(1)}, u32[]{:S(2)}, u32[]{:S(2)}) collective-permute-start(f32[3,12,16,2]{3,2,1,0:T(8,128)S(1)} %get-tuple-element.228), channel_id=1, source_target_pairs={{0,4},{1,5},{2,6},{3,7},{8,12},{9,13},{10,14},{11,15},{16,20},{17,... | collective-permute-start | bytes 13832 | tf_op jit(solution)/shard_map/ppermute | solution.py:28
  211.1 6.2 %collective-permute-start.41 = (f32[3,12,2,132]{3,2,1,0:T(2,128)S(1)}, f32[3,12,2,132]{3,2,1,0:T(2,128)S(1)}, u32[]{:S(2)}, u32[]{:S(2)}) collective-permute-start(f32[3,12,2,132]{3,2,1,0:T(2,128)S(1)} %get-tuple-element.205), channel_id=1, source_target_pairs={{1,0},{2,1},{3,2},{5,4},{6,5},{7,6},{9,8},{10,9},{11,10},{13,12},{... | collective-permute-start | bytes 114056 | tf_op jit(solution)/shard_map/ppermute | solution.py:29
  212.4 6.0 %collective-permute-start.40 = (f32[3,12,2,132]{3,2,1,0:T(2,128)S(1)}, f32[3,12,2,132]{3,2,1,0:T(2,128)S(1)}, u32[]{:S(2)}, u32[]{:S(2)}) collective-permute-start(f32[3,12,2,132]{3,2,1,0:T(2,128)S(1)} %get-tuple-element.206), channel_id=1, source_target_pairs={{0,1},{1,2},{2,3},{4,5},{5,6},{6,7},{8,9},{9,10},{10,11},{12,13},{... | collective-permute-start | bytes 114056 | tf_op jit(solution)/shard_map/ppermute | solution.py:28
  (17 other events, 108.8 us)
where the time goes:
time: 228 us; the launch traced here: 225 us
  starting transfers between devices  118 us (52%)
  waiting for transfers between devices  62.9 us (28%)
  other arithmetic  38.9 us (17%)
  local copies, waits for them, and re-layouts  3.64 us (2%)
    ppermute x21, starting transfers between devices, extended(): before = lax.ppermute(last, axis, up)  78 us
    ppermute x21, starting transfers between devices, extended(): after = lax.ppermute(first, axis, down)  40.3 us
    ppermute x21, waiting for transfers between devices, extended(): after = lax.ppermute(first, axis, down)  38.9 us
    another operation x15, other arithmetic, bond_forces(): return jnp.stack([total_x, total_y, total_z]) * valid_in  28.7 us
    ppermute x21, waiting for transfers between devices, extended(): before = lax.ppermute(last, axis, up)  24 us
    concatenate x19, other arithmetic, extended(): x = jnp.concatenate([before, x, after], axis=dim)  5.85 us
  transfers between devices with their start and end apart: 42, of which 19 were waited for; matrix products, arithmetic and copies ran while one was open for 3% of the time, Pallas kernels for 0%

commit v1 on v0

v1 whole, which is shorter than its diff:
```python
import math

import jax
import jax.numpy as jnp
from jax import lax
from jax.experimental import pallas as pl
from jax.experimental.pallas import tpu as pltpu
from jax.sharding import PartitionSpec as P

STEPS = 4
DT = 0.2
HALF = 0.1
MESH = pl.DeviceIdType.MESH

DIRS = [
    (ex, ey, ez)
    for ex in range(-2, 3)
    for ey in range(-2, 3)
    for ez in range(-2, 3)
    if 0 < ex * ex + ey * ey + ez * ez <= 4
]
WHERE = {e: n for n, e in enumerate(DIRS)}
PARTNERS = [
    (dx, dz, dy)
    for dx in (-1, 0, 1)
    for dz in (-1, 0, 1)
    for dy in (0, 1)
    if (dx, dz, dy) != (0, 0, 0)
]
SLOT = {d: n for n, d in enumerate(PARTNERS)}
NP = len(PARTNERS)
TINY = 1e-30


def opposite(d):
    return (-d[0], -d[1], d[2])


def kernel(
    table_c, table_q, u_in, v_in, class_in, clamp_in,
    u_out, v_out,
    grid, yp1, ym1, yp2, ym2, speed, cls, clm, free, acc, coef,
    zsend, zrecv, csend, crecv, qsend, qrecv,
    local_sem, send_sem, recv_sem,
):
    gx, gy, gz = lax.axis_index("gx"), lax.axis_index("gy"), lax.axis_index("gz")
    nx, nz = lax.axis_size("gx"), lax.axis_size("gz")

    def device(d):
        return {
            "gx": lax.rem(gx + (d[0] + nx), nx),
            "gz": lax.rem(gz + (d[1] + nz), nz),
            "gy": 1 - gy if d[2] else gy,
        }

    barrier = pltpu.get_barrier_semaphore()
    for d in PARTNERS:
        pl.semaphore_signal(barrier, inc=1, device_id=device(d), device_id_type=MESH)

    loads = [
        pltpu.make_async_copy(class_in, cls, local_sem.at[0]),
        pltpu.make_async_copy(u_in, grid.at[0, 0:3, 2:10, 8:24], local_sem.at[1]),
        pltpu.make_async_copy(v_in, speed, local_sem.at[2]),
        pltpu.make_async_copy(clamp_in, clm, local_sem.at[3]),
    ]
    for c in loads:
        c.start()

    lane = lax.broadcasted_iota(jnp.int32, (8, 128), 1)
    row = lax.broadcasted_iota(jnp.int32, (8, 128), 0)
    seam_from = jnp.where(gy == 1, 0, 126)
    pair = lax.rem(lane - seam_from + 128, 128) // 2
    lower = gy == 0

    seam = {
        1: (lane < 1) & lower,
        2: (lane < 2) & lower,
        -1: (lane > 126) & (gy == 1),
        -2: (lane > 125) & (gy == 1),
    }

    def transfers(s, nc, which=lambda d: True):
        out = []
        for d in PARTNERS:
            if not which(d):
                continue
            dx, dz, dy = d
            m = SLOT[d]
            o = SLOT[opposite(d)]
            if d == (-1, 0, 0):
                src, dst = grid.at[s, 0:nc, 2:4, 8:24], grid.at[s, 0:nc, 10:12, 8:24]
            elif d == (1, 0, 0):
                src, dst = grid.at[s, 0:nc, 8:10, 8:24], grid.at[s, 0:nc, 0:2, 8:24]
            elif dy == 0 and dx == 0:
                side = 0 if dz < 0 else 1
                src, dst = zsend.at[side, 0:nc], zrecv.at[s, 1 - side, 0:nc]
            elif dy == 0:
                q = (0 if dx < 0 else 2) + (0 if dz < 0 else 1)
                src, dst = csend.at[q], crecv.at[s, 3 - q]
            else:
                if dz == 0:
                    src, dst = qsend.at[...], qrecv.at[s, 1 - dx, 8:24]
                elif dz > 0:
                    src, dst = qsend.at[8:16], qrecv.at[s, 1 - dx, 0:8]
                else:
                    src, dst = qsend.at[0:8], qrecv.at[s, 1 - dx, 24:32]
            out.append(
                pltpu.make_async_remote_copy(
                    src_ref=src,
                    dst_ref=dst,
                    send_sem=send_sem.at[m],
                    recv_sem=recv_sem.at[s, o],
                    device_id=device(d),
                    device_id_type=MESH,
                )
            )
        return out

    def send_all(s, nc):
        for t in transfers(s, nc):
            t.start()

    def wait_sent(s, nc):
        for t in transfers(s, nc):
            t.wait_send()

    def wait_from(s, nc, which):
        for t in transfers(s, nc, which):
            t.wait_recv()

    def pack(s, planes, nc, fresh):
        for t in range(2):
            packed = None if fresh else qsend[8 * t : 8 * t + 8, :]
            for c in range(nc):
                for p in planes:
                    k = c * 8 + p
                    tile = grid[s, c, p + 2, 8 + 8 * t : 16 + 8 * t, :]
                    moved = pltpu.roll(tile, 2 * k, 1) if k else tile
                    packed = moved if packed is None else jnp.where(pair == k, moved, packed)
            qsend[8 * t : 8 * t + 8, :] = packed
        for c in range(nc):
            for p in planes:
                at = 2 * (p % 4)
                zsend[0, c, p // 4, at : at + 2, :] = grid[s, c, p + 2, 8:10, :]
                zsend[1, c, p // 4, at : at + 2, :] = grid[s, c, p + 2, 22:24, :]
            if 0 in planes:
                csend[0, c : c + 1, :] = grid[s, c, 2, 8:9, :]
                csend[1, c : c + 1, :] = grid[s, c, 2, 23:24, :]
            if 7 in planes:
                csend[2, c : c + 1, :] = grid[s, c, 9, 8:9, :]
                csend[3, c : c + 1, :] = grid[s, c, 9, 23:24, :]

    def shifted(s, p, nc):
        own = 0 <= p < 8
        slot, plane = (1, p) if own else ((0, 7) if p < 0 else (2, 0))
        for c in range(nc):
            k = c * 8 + plane
            for r in range(4):
                rows = slice(8 * r, 8 * r + 8)
                tile = grid[s, c, p + 2, rows, :]
                other = qrecv[s, slot, rows, :]
                if k:
                    other = pltpu.roll(other, 128 - 2 * k, 1)
                yp1[c, p + 2, rows, :] = pltpu.roll(jnp.where(seam[1], other, tile), 127, 1)
                ym1[c, p + 2, rows, :] = pltpu.roll(jnp.where(seam[-1], other, tile), 1, 1)
                if own and r in (1, 2):
                    yp2[c, p + 2, rows, :] = pltpu.roll(jnp.where(seam[2], other, tile), 126, 1)
                    ym2[c, p + 2, rows, :] = pltpu.roll(jnp.where(seam[-2], other, tile), 2, 1)

    def spread_near(s, nc):
        for c in range(nc):
            for p in range(8):
                at = 2 * (p % 4)
                grid[s, c, p + 2, 6:8, :] = zrecv[s, 0, c, p // 4, at : at + 2, :]
                grid[s, c, p + 2, 24:26, :] = zrecv[s, 1, c, p // 4, at : at + 2, :]
        for p in range(8):
            shifted(s, p, nc)

    def spread_far(s, nc):
        for c in range(nc):
            grid[s, c, 1, 7:8, :] = crecv[s, 0, c : c + 1, :]
            grid[s, c, 1, 24:25, :] = crecv[s, 1, c : c + 1, :]
            grid[s, c, 10, 7:8, :] = crecv[s, 2, c : c + 1, :]
            grid[s, c, 10, 24:25, :] = crecv[s, 3, c : c + 1, :]
        for p in (-1, 8):
            shifted(s, p, nc)

    def bonds(s, p, dirs, first, onto, x_inside=None):
        for t in range(2):
            mine = slice(8 * t, 8 * t + 8)
            base = slice(8 + 8 * t, 16 + 8 * t)
            centre = [grid[s, c, p + 2, base, :] for c in range(3)]
            moved = {}
            for c in range(3):
                for e in range(-2, 3):
                    moved[c, e] = centre[c] - float(e) if e else centre[c]
            if first:
                own_c, own_q = grid[s, 3, p + 2, base, :], grid[s, 4, p + 2, base, :]
            total = [acc[c, p, mine, :] for c in range(3)] if onto else [None] * 3
            for e in dirs:
                ex, ey, ez = e
                length = math.sqrt(ex * ex + ey * ey + ez * ez)
                rows = slice(8 + 8 * t + ez, 16 + 8 * t + ez)
                field = {1: yp1, -1: ym1, 2: yp2, -2: ym2}.get(ey)

                def near(c):
                    if field is None:
                        return grid[s, c, p + 2 + ex, rows, :]
                    return field[c, p + 2 + ex, rows, :]

                n = WHERE[e]
                if first:
                    a = (own_c + near(3)) * (0.5 / (length * length))
                    if x_inside is not None:
                        a = a * x_inside
                    if ey:
                        here = lane + (128 * gy + ey)
                        a = jnp.where((here >= 0) & (here < 256), a, 0.0)
                    if (t == 0 and ez < 0) or (t == 1 and ez > 0):
                        here = row + (16 * gz + 8 * t + ez)
                        a = jnp.where((here >= 0) & (here < 16 * nz), a, 0.0)
                    b = (-2.0 / (length * math.log(2.0))) / (own_q + near(4))
                    coef[n, 0, p, mine, :] = a
                    coef[n, 1, p, mine, :] = b
                else:
                    a = coef[n, 0, p, mine, :]
                    b = coef[n, 1, p, mine, :]
                sx = near(0) - moved[0, ex]
                sy = near(1) - moved[1, ey]
                sz = near(2) - moved[2, ez]
                square = jnp.maximum(sx * sx + sy * sy + sz * sz, TINY)
                inverse = lax.rsqrt(square)
                over = square * inverse - length
                pull = (a * over) * inverse * jnp.exp2(b * jnp.abs(over))
                for c, part in enumerate((sx, sy, sz)):
                    add = pull * part
                    total[c] = add if total[c] is None else total[c] + add
            for c in range(3):
                acc[c, p, mine, :] = total[c]

    inner = {
        0: [e for e in DIRS if e[0] >= 0],
        1: [e for e in DIRS if e[0] >= -1],
        6: [e for e in DIRS if e[0] <= 1],
        7: [e for e in DIRS if e[0] <= 0],
    }

    def near_bonds(s, first):
        for p in (0, 1, 6, 7):
            bonds(s, p, inner[p], first, False)

        def middle(p, carry):
            bonds(s, p, DIRS, first, False)
            return carry

        lax.fori_loop(2, 6, middle, 0)

    def far_bonds(s, first):
        for p in (0, 1, 6, 7):
            inside = None
            if first:
                inside = jnp.where(gx > 0, 1.0, 0.0) if p < 2 else jnp.where(gx < nx - 1, 1.0, 0.0)
            bonds(s, p, [e for e in DIRS if e not in inner[p]], first, True, inside)

    def advance(s, planes, weight):
        for p in planes:
            for c in range(3):
                new = free[p] * (speed[c, p] + weight * acc[c, p])
                speed[c, p] = new
                grid[1 - s, c, p + 2, 8:24, :] = grid[s, c, p + 2, 8:24, :] + DT * new

    near_by = lambda d: d[0] == 0
    far_off = lambda d: d[0] != 0

    loads[0].wait()
    for p in range(8):
        kind = cls[p]
        c_of = jnp.where(kind == 1, table_c[1], table_c[0])
        c_of = jnp.where(kind == 2, table_c[2], c_of)
        c_of = jnp.where(kind == 3, table_c[3], c_of)
        q_of = jnp.where(kind == 1, table_q[1], table_q[0])
        q_of = jnp.where(kind == 2, table_q[2], q_of)
        q_of = jnp.where(kind == 3, table_q[3], q_of)
        grid[0, 3, p + 2, 8:24, :] = c_of
        grid[0, 4, p + 2, 8:24, :] = q_of
    loads[1].wait()
    pack(0, range(8), 5, True)
    pl.semaphore_wait(barrier, NP)
    send_all(0, 5)
    loads[2].wait()
    loads[3].wait()
    for p in range(8):
        free[p] = 1.0 - clm[p].astype(jnp.float32)

    wait_from(0, 5, near_by)
    spread_near(0, 5)
    near_bonds(0, True)
    advance(0, range(2, 6), HALF)
    wait_sent(0, 5)
    pack(1, range(2, 6), 3, True)
    wait_from(0, 5, far_off)
    spread_far(0, 5)
    far_bonds(0, True)
    advance(0, (0, 1, 6, 7), HALF)
    pack(1, (0, 1, 6, 7), 3, False)
    send_all(1, 3)

    def step(k, carry):
        s = lax.rem(k, 2)
        weight = jnp.where(k == STEPS, HALF, DT)
        wait_from(s, 3, near_by)
        spread_near(s, 3)
        near_bonds(s, False)
        advance(s, range(2, 6), weight)
        wait_sent(s, 3)
        pack(1 - s, range(2, 6), 3, True)
        wait_from(s, 3, far_off)
        spread_far(s, 3)
        far_bonds(s, False)
        advance(s, (0, 1, 6, 7), weight)
        pack(1 - s, (0, 1, 6, 7), 3, False)

        @pl.when(k < STEPS)
        def _():
            send_all(1 - s, 3)

        return carry

    lax.fori_loop(1, STEPS + 1, step, 0)

    stores = [
        pltpu.make_async_copy(grid.at[STEPS % 2, 0:3, 2:10, 8:24], u_out, local_sem.at[1]),
        pltpu.make_async_copy(speed, v_out, local_sem.at[2]),
    ]
    for c in stores:
        c.start()
    for c in stores:
        c.wait()


def local(displacement, velocity, classes, clamped, stiffness, softening):
    block = displacement.shape
    f32 = jnp.float32
    anywhere = pl.BlockSpec(memory_space=pl.ANY)
    scalars = pl.BlockSpec(memory_space=pltpu.SMEM)
    return pl.pallas_call(
        kernel,
        out_shape=[jax.ShapeDtypeStruct(block, f32)] * 2,
        in_specs=[scalars, scalars] + [anywhere] * 4,
        out_specs=[anywhere] * 2,
        scratch_shapes=[
            pltpu.VMEM((2, 5, 12, 32, 128), f32),
            pltpu.VMEM((5, 12, 32, 128), f32),
            pltpu.VMEM((5, 12, 32, 128), f32),
            pltpu.VMEM((5, 12, 32, 128), f32),
            pltpu.VMEM((5, 12, 32, 128), f32),
            pltpu.VMEM((3, 8, 16, 128), f32),
            pltpu.VMEM((8, 16, 128), jnp.int32),
            pltpu.VMEM((8, 16, 128), jnp.int32),
            pltpu.VMEM((8, 16, 128), f32),
            pltpu.VMEM((3, 8, 16, 128), f32),
            pltpu.VMEM((len(DIRS), 2, 8, 16, 128), f32),
            pltpu.VMEM((2, 5, 2, 8, 128), f32),
            pltpu.VMEM((2, 2, 5, 2, 8, 128), f32),
            pltpu.VMEM((4, 8, 128), f32),
            pltpu.VMEM((2, 4, 8, 128), f32),
            pltpu.VMEM((16, 128), f32),
            pltpu.VMEM((2, 3, 32, 128), f32),
            pltpu.SemaphoreType.DMA((4,)),
            pltpu.SemaphoreType.DMA((NP,)),
            pltpu.SemaphoreType.DMA((2, NP)),
        ],
        compiler_params=pltpu.CompilerParams(collective_id=0, has_side_effects=True),
    )(stiffness, softening, displacement, velocity, classes, clamped)


def solution(mesh):
    return jax.shard_map(
        local,
        mesh=mesh,
        in_specs=(
            P(None, "gx", "gz", "gy"),
            P(None, "gx", "gz", "gy"),
            P("gx", "gz", "gy"),
            P("gx", "gz", "gy"),
            P(),
            P(),
        ),
        out_specs=(P(None, "gx", "gz", "gy"), P(None, "gx", "gz", "gy")),
        check_vma=False,
    )
```

time: 228 us -> 67.2 us (0.29)
  the two profiles are of different devices: /device:TPU:121 before, /device:TPU:8 now
where the time goes in v1:
time: 67.2 us; the launch traced here: 67.1 us
  Pallas kernels  64.1 us (95%)
  local copies, waits for them, and re-layouts  2.34 us (3%)
    pallas_call x1, Pallas kernels, local(): pl.pallas_call(kernel, out_shape=[jax.ShapeDtypeStruct(block, f32)] * 2,...  64.1 us
    unnamed x4, local copies, waits for them, and re-layouts  2.34 us

profile of v1, /device:TPU:8, one launch (start us, length us, event | category | flops | bytes accessed | tf_op | source)
XLA Modules:
  0.0 67.1 jit_solution(6655893141839115140)
XLA Ops:
  0.6 64.1 %shard_map.77 = (f32[3,8,16,128]{3,2,1,0:T(8,128)}, f32[3,8,16,128]{3,2,1,0:T(8,128)}) custom-call(f32[4]{0:T(128)} %table_c.1, f32[4]{0:T(128)} %table_q.1, f32[3,8,16,128]{3,2,1,0:T(8,128)} %u_in.1, f32[3,8,16,128]{3,2,1,0:T(8,128)} %v_in.1, s32[8,16,128]{2,1,0:T(8,128)} %class_in.1, s32[8,16,128]{2,1,0:T(8,128)} %clamp_in.1), custom_call_target="tpu_custom_call" | custom-call | tf_op jit(solution)/shard_map/pallas_call | solution.py:346
  64.7 0.0 copy-start
  64.7 1.7 %copy.10 = f32[3,8,16,128]{3,2,1,0:T(8,128)} copy(f32[3,8,16,128]{3,2,1,0:T(8,128)} %get-tuple-element.4) | data formatting | bytes 393216
  66.4 0.0 copy-done
  66.4 0.7 %copy.11 = f32[3,8,16,128]{3,2,1,0:T(8,128)} copy(f32[3,8,16,128]{3,2,1,0:T(8,128)S(1)} %copy-done) | data formatting | bytes 393216
Async XLA Ops:
  64.7 1.7 %copy-start = (f32[3,8,16,128]{3,2,1,0:T(8,128)S(1)}, f32[3,8,16,128]{3,2,1,0:T(8,128)}, u32[]{:S(2)}) copy-start(f32[3,8,16,128]{3,2,1,0:T(8,128)} %get-tuple-element.5) | copy-start | bytes 589828

commit v2 on v1

--- a/solution.py
+++ b/solution.py
@@ -39,7 +39,7 @@
 def kernel(
     table_c, table_q, u_in, v_in, class_in, clamp_in,
     u_out, v_out,
-    grid, yp1, ym1, yp2, ym2, speed, cls, clm, free, acc, coef,
+    grid, turned, speed, cls, clm, free, acc, coef,
     zsend, zrecv, csend, crecv, qsend, qrecv,
     local_sem, send_sem, recv_sem,
 ):
@@ -53,9 +53,35 @@
             "gy": 1 - gy if d[2] else gy,
         }
 
+    has_left, has_right = gx > 0, gx < nx - 1
+
+    def by_side(left, beside, right):
+        pl.when(has_left)(left)
+        beside()
+        pl.when(has_right)(right)
+
+    zero = jnp.zeros((8, 128), jnp.float32)
+    for par in range(2):
+        for r in range(4):
+            rows = slice(8 * r, 8 * r + 8)
+            for c in range(5):
+                for plane in (0, 1, 10, 11):
+                    grid[par, c, plane, rows, :] = zero
+            qrecv[par, 0, rows, :] = zero
+            qrecv[par, 2, rows, :] = zero
+            crecv[par, r] = zero
+
     barrier = pltpu.get_barrier_semaphore()
-    for d in PARTNERS:
-        pl.semaphore_signal(barrier, inc=1, device_id=device(d), device_id_type=MESH)
+
+    def greet(dx):
+        def go():
+            for d in PARTNERS:
+                if d[0] == dx:
+                    pl.semaphore_signal(barrier, inc=1, device_id=device(d), device_id_type=MESH)
+
+        return go
+
+    by_side(greet(-1), greet(0), greet(1))
 
     loads = [
         pltpu.make_async_copy(class_in, cls, local_sem.at[0]),
@@ -68,16 +94,13 @@
 
     lane = lax.broadcasted_iota(jnp.int32, (8, 128), 1)
     row = lax.broadcasted_iota(jnp.int32, (8, 128), 0)
-    seam_from = jnp.where(gy == 1, 0, 126)
-    pair = lax.rem(lane - seam_from + 128, 128) // 2
-    lower = gy == 0
-
-    seam = {
-        1: (lane < 1) & lower,
-        2: (lane < 2) & lower,
-        -1: (lane > 126) & (gy == 1),
-        -2: (lane > 125) & (gy == 1),
+    upper = gy == 1
+    pair = lax.rem(lane - jnp.where(upper, 0, 126) + 128, 128) // 2
+    from_other = {
+        1: lane == jnp.where(upper, 0, 127),
+        2: (lane >= jnp.where(upper, 0, 126)) & (lane < jnp.where(upper, 2, 128)),
     }
+    swing = {1: jnp.where(upper, 1, 127), 2: jnp.where(upper, 2, 126)}
 
     def transfers(s, nc, which=lambda d: True):
         out = []
@@ -116,19 +139,39 @@
             )
         return out
 
-    def send_all(s, nc):
-        for t in transfers(s, nc):
-            t.start()
+    def each(s, nc, which, act):
+        for t in transfers(s, nc, which):
+            act(t)
+
+    def start(s, nc, which):
+        by_side(
+            lambda: each(s, nc, lambda d: d[0] == -1 and which(d), lambda t: t.start()),
+            lambda: each(s, nc, lambda d: d[0] == 0 and which(d), lambda t: t.start()),
+            lambda: each(s, nc, lambda d: d[0] == 1 and which(d), lambda t: t.start()),
+        )
 
     def wait_sent(s, nc):
-        for t in transfers(s, nc):
-            t.wait_send()
-
-    def wait_from(s, nc, which):
-        for t in transfers(s, nc, which):
-            t.wait_recv()
-
-    def pack(s, planes, nc, fresh):
+        by_side(
+            lambda: each(s, nc, lambda d: d[0] == -1, lambda t: t.wait_send()),
+            lambda: each(s, nc, lambda d: d[0] == 0, lambda t: t.wait_send()),
+            lambda: each(s, nc, lambda d: d[0] == 1, lambda t: t.wait_send()),
+        )
+
+    def wait_near(s, nc):
+        each(s, nc, lambda d: d[0] == 0, lambda t: t.wait_recv())
+
+    def wait_far(s, nc):
+        pl.when(has_left)(lambda: each(s, nc, lambda d: d[0] == 1, lambda t: t.wait_recv()))
+        pl.when(has_right)(lambda: each(s, nc, lambda d: d[0] == -1, lambda t: t.wait_recv()))
+
+    def pack_corners(s, nc):
+        for c in range(nc):
+            csend[0, c : c + 1, :] = grid[s, c, 2, 8:9, :]
+            csend[1, c : c + 1, :] = grid[s, c, 2, 23:24, :]
+            csend[2, c : c + 1, :] = grid[s, c, 9, 8:9, :]
+            csend[3, c : c + 1, :] = grid[s, c, 9, 23:24, :]
+
+    def pack_columns(s, planes, nc, fresh):
         for t in range(2):
             packed = None if fresh else qsend[8 * t : 8 * t + 8, :]
             for c in range(nc):
@@ -138,34 +181,55 @@
                     moved = pltpu.roll(tile, 2 * k, 1) if k else tile
                     packed = moved if packed is None else jnp.where(pair == k, moved, packed)
             qsend[8 * t : 8 * t + 8, :] = packed
+
+    def pack_rows(s, planes, nc):
         for c in range(nc):
             for p in planes:
                 at = 2 * (p % 4)
                 zsend[0, c, p // 4, at : at + 2, :] = grid[s, c, p + 2, 8:10, :]
                 zsend[1, c, p // 4, at : at + 2, :] = grid[s, c, p + 2, 22:24, :]
-            if 0 in planes:
-                csend[0, c : c + 1, :] = grid[s, c, 2, 8:9, :]
-                csend[1, c : c + 1, :] = grid[s, c, 2, 23:24, :]
-            if 7 in planes:
-                csend[2, c : c + 1, :] = grid[s, c, 9, 8:9, :]
-                csend[3, c : c + 1, :] = grid[s, c, 9, 23:24, :]
-
-    def shifted(s, p, nc):
-        own = 0 <= p < 8
-        slot, plane = (1, p) if own else ((0, 7) if p < 0 else (2, 0))
-        for c in range(nc):
-            k = c * 8 + plane
-            for r in range(4):
-                rows = slice(8 * r, 8 * r + 8)
-                tile = grid[s, c, p + 2, rows, :]
-                other = qrecv[s, slot, rows, :]
-                if k:
-                    other = pltpu.roll(other, 128 - 2 * k, 1)
-                yp1[c, p + 2, rows, :] = pltpu.roll(jnp.where(seam[1], other, tile), 127, 1)
-                ym1[c, p + 2, rows, :] = pltpu.roll(jnp.where(seam[-1], other, tile), 1, 1)
-                if own and r in (1, 2):
-                    yp2[c, p + 2, rows, :] = pltpu.roll(jnp.where(seam[2], other, tile), 126, 1)
-                    ym2[c, p + 2, rows, :] = pltpu.roll(jnp.where(seam[-2], other, tile), 2, 1)
+
+    SHIFTS = ((0, 127), (1, 1), (2, 126), (3, 2))
+
+    def turn_own(s, planes, nc, far):
+        for c in range(nc):
+            for p in planes:
+                for r in (1, 2):
+                    rows = slice(8 * r, 8 * r + 8)
+                    tile = grid[s, c, p + 2, rows, :]
+                    for n, by in SHIFTS[:2] if far else SHIFTS:
+                        turned[n, c, p + 2, rows, :] = pltpu.roll(tile, by, 1)
+
+    def turn_rows(s, planes, nc):
+        for c in range(nc):
+            for p in planes:
+                ends = jnp.where(row < 4, grid[s, c, p + 2, 24:32, :], grid[s, c, p + 2, 0:8, :])
+                for n, by in SHIFTS[:2]:
+                    moved = pltpu.roll(ends, by, 1)
+                    turned[n, c, p + 2, 0:8, :] = moved
+                    turned[n, c, p + 2, 24:32, :] = moved
+
+    def close_seam(s, planes, nc):
+        for c in range(nc):
+            for p in planes:
+                slot, plane = (1, p) if 0 <= p < 8 else ((0, 7) if p < 0 else (2, 0))
+                k = c * 8 + plane
+
+                def other(tile, step):
+                    return pltpu.roll(tile, lax.rem(swing[step] + (256 - 2 * k), 128), 1)
+
+                ends = jnp.where(row < 4, qrecv[s, slot, 24:32, :], qrecv[s, slot, 0:8, :])
+                ends = other(ends, 1)
+                for r in range(4):
+                    rows = slice(8 * r, 8 * r + 8)
+                    inner_rows = r in (1, 2)
+                    here = turned[gy, c, p + 2, rows, :]
+                    there = other(qrecv[s, slot, rows, :], 1) if inner_rows else ends
+                    turned[gy, c, p + 2, rows, :] = jnp.where(from_other[1], there, here)
+                    if inner_rows and slot == 1:
+                        here = turned[2 + gy, c, p + 2, rows, :]
+                        there = other(qrecv[s, slot, rows, :], 2)
+                        turned[2 + gy, c, p + 2, rows, :] = jnp.where(from_other[2], there, here)
 
     def spread_near(s, nc):
         for c in range(nc):
@@ -173,8 +237,8 @@
                 at = 2 * (p % 4)
                 grid[s, c, p + 2, 6:8, :] = zrecv[s, 0, c, p // 4, at : at + 2, :]
                 grid[s, c, p + 2, 24:26, :] = zrecv[s, 1, c, p // 4, at : at + 2, :]
-        for p in range(8):
-            shifted(s, p, nc)
+        turn_rows(s, range(8), nc)
+        close_seam(s, range(8), nc)
 
     def spread_far(s, nc):
         for c in range(nc):
@@ -182,11 +246,16 @@
             grid[s, c, 1, 24:25, :] = crecv[s, 1, c : c + 1, :]
             grid[s, c, 10, 7:8, :] = crecv[s, 2, c : c + 1, :]
             grid[s, c, 10, 24:25, :] = crecv[s, 3, c : c + 1, :]
-        for p in (-1, 8):
-            shifted(s, p, nc)
-
-    def bonds(s, p, dirs, first, onto, x_inside=None):
+        turn_own(s, (-1, 8), nc, True)
+        turn_rows(s, (-1, 8), nc)
+        close_seam(s, (-1, 8), nc)
+
+    def needs_near(e, t):
+        return bool(e[1]) or (t == 0 and e[2] < 0) or (t == 1 and e[2] > 0)
+
+    def bonds(s, p, dirs, first, onto, x_inside=None, part=None):
         for t in range(2):
+            chosen = [e for e in dirs if part is None or needs_near(e, t) == part]
             mine = slice(8 * t, 8 * t + 8)
             base = slice(8 + 8 * t, 16 + 8 * t)
             centre = [grid[s, c, p + 2, base, :] for c in range(3)]
@@ -197,16 +266,16 @@
             if first:
                 own_c, own_q = grid[s, 3, p + 2, base, :], grid[s, 4, p + 2, base, :]
             total = [acc[c, p, mine, :] for c in range(3)] if onto else [None] * 3
-            for e in dirs:
+            for e in chosen:
                 ex, ey, ez = e
                 length = math.sqrt(ex * ex + ey * ey + ez * ez)
                 rows = slice(8 + 8 * t + ez, 16 + 8 * t + ez)
-                field = {1: yp1, -1: ym1, 2: yp2, -2: ym2}.get(ey)
+                field = {1: 0, -1: 1, 2: 2, -2: 3}.get(ey)
 
                 def near(c):
                     if field is None:
                         return grid[s, c, p + 2 + ex, rows, :]
-                    return field[c, p + 2 + ex, rows, :]
+                    return turned[field, c, p + 2 + ex, rows, :]
 
                 n = WHERE[e]
                 if first:
@@ -232,8 +301,8 @@
                 inverse = lax.rsqrt(square)
                 over = square * inverse - length
                 pull = (a * over) * inverse * jnp.exp2(b * jnp.abs(over))
-                for c, part in enumerate((sx, sy, sz)):
-                    add = pull * part
+                for c, way in enumerate((sx, sy, sz)):
+                    add = pull * way
                     total[c] = add if total[c] is None else total[c] + add
             for c in range(3):
                 acc[c, p, mine, :] = total[c]
@@ -245,12 +314,12 @@
         7: [e for e in DIRS if e[0] <= 0],
     }
 
-    def near_bonds(s, first):
+    def near_bonds(s, first, part):
         for p in (0, 1, 6, 7):
-            bonds(s, p, inner[p], first, False)
+            bonds(s, p, inner[p], first, part, part=part)
 
         def middle(p, carry):
-            bonds(s, p, DIRS, first, False)
+            bonds(s, p, DIRS, first, part, part=part)
             return carry
 
         lax.fori_loop(2, 6, middle, 0)
@@ -269,8 +338,28 @@
                 speed[c, p] = new
                 grid[1 - s, c, p + 2, 8:24, :] = grid[s, c, p + 2, 8:24, :] + DT * new
 
-    near_by = lambda d: d[0] == 0
-    far_off = lambda d: d[0] != 0
+    def send(s, nc):
+        pack_corners(s, nc)
+        start(s, nc, lambda d: d[2] == 0 and d[0])
+        pack_columns(s, (0, 1, 6, 7), nc, False)
+        start(s, nc, lambda d: d[2] == 1)
+        pack_rows(s, (0, 1, 6, 7), nc)
+        start(s, nc, lambda d: d[2] == 0 and not d[0])
+
+    def run(s, nc, first, weight, go_on):
+        turn_own(s, range(8), nc, False)
+        near_bonds(s, first, False)
+        wait_near(s, nc)
+        spread_near(s, nc)
+        near_bonds(s, first, True)
+        advance(s, range(2, 6), weight)
+        wait_sent(s, nc)
+        go_on(lambda: (pack_columns(1 - s, range(2, 6), 3, True), pack_rows(1 - s, range(2, 6), 3)))
+        wait_far(s, nc)
+        spread_far(s, nc)
+        far_bonds(s, first)
+        advance(s, (0, 1, 6, 7), weight)
+        go_on(lambda: send(1 - s, 3))
 
     loads[0].wait()
     for p in range(8):
@@ -284,46 +373,26 @@
         grid[0, 3, p + 2, 8:24, :] = c_of
         grid[0, 4, p + 2, 8:24, :] = q_of
     loads[1].wait()
-    pack(0, range(8), 5, True)
-    pl.semaphore_wait(barrier, NP)
-    send_all(0, 5)
+    pack_columns(0, range(2, 6), 5, True)
+    pack_rows(0, range(2, 6), 5)
+    pl.semaphore_wait(barrier, 5 + jnp.where(has_left, 6, 0) + jnp.where(has_right, 6, 0))
+    send(0, 5)
     loads[2].wait()
     loads[3].wait()
     for p in range(8):
         free[p] = 1.0 - clm[p].astype(jnp.float32)
 
-    wait_from(0, 5, near_by)
-    spread_near(0, 5)
-    near_bonds(0, True)
-    advance(0, range(2, 6), HALF)
-    wait_sent(0, 5)
-    pack(1, range(2, 6), 3, True)
-    wait_from(0, 5, far_off)
-    spread_far(0, 5)
-    far_bonds(0, True)
-    advance(0, (0, 1, 6, 7), HALF)
-    pack(1, (0, 1, 6, 7), 3, False)
-    send_all(1, 3)
+    run(0, 5, True, HALF, lambda f: f())
 
     def step(k, carry):
-        s = lax.rem(k, 2)
         weight = jnp.where(k == STEPS, HALF, DT)
-        wait_from(s, 3, near_by)
-        spread_near(s, 3)
-        near_bonds(s, False)
-        advance(s, range(2, 6), weight)
-        wait_sent(s, 3)
-        pack(1 - s, range(2, 6), 3, True)
-        wait_from(s, 3, far_off)
-        spread_far(s, 3)
-        far_bonds(s, False)
-        advance(s, (0, 1, 6, 7), weight)
-        pack(1 - s, (0, 1, 6, 7), 3, False)
-
-        @pl.when(k < STEPS)
-        def _():
-            send_all(1 - s, 3)
-
+
+        def go_on(f):
+            @pl.when(k < STEPS)
+            def _():
+                f()
+
+        run(lax.rem(k, 2), 3, False, weight, go_on)
         return carry
 
     lax.fori_loop(1, STEPS + 1, step, 0)
@@ -350,10 +419,7 @@
         out_specs=[anywhere] * 2,
         scratch_shapes=[
             pltpu.VMEM((2, 5, 12, 32, 128), f32),
-            pltpu.VMEM((5, 12, 32, 128), f32),
-            pltpu.VMEM((5, 12, 32, 128), f32),
-            pltpu.VMEM((5, 12, 32, 128), f32),
-            pltpu.VMEM((5, 12, 32, 128), f32),
+            pltpu.VMEM((4, 5, 12, 32, 128), f32),
             pltpu.VMEM((3, 8, 16, 128), f32),
             pltpu.VMEM((8, 16, 128), jnp.int32),
             pltpu.VMEM((8, 16, 128), jnp.int32),

time: 67.2 us -> 41.3 us (0.61)
  the two profiles are of different devices: /device:TPU:8 before, /device:TPU:121 now
where the time goes in v2:
time: 41.3 us; the launch traced here: 41.2 us
  Pallas kernels  38.2 us (92%)
  local copies, waits for them, and re-layouts  2.34 us (6%)
  between operations  0.65 us (2%)
    pallas_call x1, Pallas kernels, local(): pl.pallas_call(kernel, out_shape=[jax.ShapeDtypeStruct(block, f32)] * 2,...  38.2 us
    unnamed x4, local copies, waits for them, and re-layouts  2.34 us

profile of v2, /device:TPU:121, one launch (start us, length us, event | category | flops | bytes accessed | tf_op | source)
XLA Modules:
  0.0 41.2 jit_solution(7092689154044539149)
XLA Ops:
  0.6 38.2 %shard_map.77 = (f32[3,8,16,128]{3,2,1,0:T(8,128)}, f32[3,8,16,128]{3,2,1,0:T(8,128)}) custom-call(f32[4]{0:T(128)} %table_c.1, f32[4]{0:T(128)} %table_q.1, f32[3,8,16,128]{3,2,1,0:T(8,128)} %u_in.1, f32[3,8,16,128]{3,2,1,0:T(8,128)} %v_in.1, s32[8,16,128]{2,1,0:T(8,128)} %class_in.1, s32[8,16,128]{2,1,0:T(8,128)} %clamp_in.1), custom_call_target="tpu_custom_call" | custom-call | tf_op jit(solution)/shard_map/pallas_call | solution.py:415
  38.9 0.0 copy-start
  38.9 1.7 %copy.10 = f32[3,8,16,128]{3,2,1,0:T(8,128)} copy(f32[3,8,16,128]{3,2,1,0:T(8,128)} %get-tuple-element.4) | data formatting | bytes 393216
  40.5 0.0 copy-done
  40.5 0.7 %copy.11 = f32[3,8,16,128]{3,2,1,0:T(8,128)} copy(f32[3,8,16,128]{3,2,1,0:T(8,128)S(1)} %copy-done) | data formatting | bytes 393216
Async XLA Ops:
  38.9 1.7 %copy-start = (f32[3,8,16,128]{3,2,1,0:T(8,128)S(1)}, f32[3,8,16,128]{3,2,1,0:T(8,128)}, u32[]{:S(2)}) copy-start(f32[3,8,16,128]{3,2,1,0:T(8,128)} %get-tuple-element.5) | copy-start | bytes 589828

commit v3 on v2

--- a/solution.py
+++ b/solution.py
@@ -37,9 +37,9 @@
 
 
 def kernel(
-    table_c, table_q, u_in, v_in, class_in, clamp_in,
+    table_c_in, table_q_in, u_in, v_in, class_in, clamp_in,
     u_out, v_out,
-    grid, turned, speed, cls, clm, free, acc, coef,
+    table_c, table_q, grid, turned, speed, cls, clm, free, acc, coef,
     zsend, zrecv, csend, crecv, qsend, qrecv,
     local_sem, send_sem, recv_sem,
 ):
@@ -88,6 +88,8 @@
         pltpu.make_async_copy(u_in, grid.at[0, 0:3, 2:10, 8:24], local_sem.at[1]),
         pltpu.make_async_copy(v_in, speed, local_sem.at[2]),
         pltpu.make_async_copy(clamp_in, clm, local_sem.at[3]),
+        pltpu.make_async_copy(table_c_in, table_c, local_sem.at[4]),
+        pltpu.make_async_copy(table_q_in, table_q, local_sem.at[5]),
     ]
     for c in loads:
         c.start()
@@ -144,11 +146,13 @@
             act(t)
 
     def start(s, nc, which):
-        by_side(
-            lambda: each(s, nc, lambda d: d[0] == -1 and which(d), lambda t: t.start()),
-            lambda: each(s, nc, lambda d: d[0] == 0 and which(d), lambda t: t.start()),
-            lambda: each(s, nc, lambda d: d[0] == 1 and which(d), lambda t: t.start()),
-        )
+        def go(dx):
+            return lambda: each(s, nc, lambda d: d[0] == dx and which(d), lambda t: t.start())
+
+        if any(d[0] and which(d) for d in PARTNERS):
+            by_side(go(-1), go(0), go(1))
+        else:
+            go(0)()
 
     def wait_sent(s, nc):
         by_side(
@@ -157,8 +161,11 @@
             lambda: each(s, nc, lambda d: d[0] == 1, lambda t: t.wait_send()),
         )
 
-    def wait_near(s, nc):
-        each(s, nc, lambda d: d[0] == 0, lambda t: t.wait_recv())
+    def wait_beside(s, nc):
+        each(s, nc, lambda d: d == (0, 0, 1), lambda t: t.wait_recv())
+
+    def wait_rows(s, nc):
+        each(s, nc, lambda d: d[0] == 0 and d[1], lambda t: t.wait_recv())
 
     def wait_far(s, nc):
         pl.when(has_left)(lambda: each(s, nc, lambda d: d[0] == 1, lambda t: t.wait_recv()))
@@ -209,7 +216,7 @@
                     turned[n, c, p + 2, 0:8, :] = moved
                     turned[n, c, p + 2, 24:32, :] = moved
 
-    def close_seam(s, planes, nc):
+    def close_seam(s, planes, nc, tiles=(0, 1, 2, 3)):
         for c in range(nc):
             for p in planes:
                 slot, plane = (1, p) if 0 <= p < 8 else ((0, 7) if p < 0 else (2, 0))
@@ -218,9 +225,10 @@
                 def other(tile, step):
                     return pltpu.roll(tile, lax.rem(swing[step] + (256 - 2 * k), 128), 1)
 
-                ends = jnp.where(row < 4, qrecv[s, slot, 24:32, :], qrecv[s, slot, 0:8, :])
-                ends = other(ends, 1)
-                for r in range(4):
+                if 0 in tiles:
+                    ends = jnp.where(row < 4, qrecv[s, slot, 24:32, :], qrecv[s, slot, 0:8, :])
+                    ends = other(ends, 1)
+                for r in tiles:
                     rows = slice(8 * r, 8 * r + 8)
                     inner_rows = r in (1, 2)
                     here = turned[gy, c, p + 2, rows, :]
@@ -238,7 +246,7 @@
                 grid[s, c, p + 2, 6:8, :] = zrecv[s, 0, c, p // 4, at : at + 2, :]
                 grid[s, c, p + 2, 24:26, :] = zrecv[s, 1, c, p // 4, at : at + 2, :]
         turn_rows(s, range(8), nc)
-        close_seam(s, range(8), nc)
+        close_seam(s, range(8), nc, (0, 3))
 
     def spread_far(s, nc):
         for c in range(nc):
@@ -251,7 +259,7 @@
         close_seam(s, (-1, 8), nc)
 
     def needs_near(e, t):
-        return bool(e[1]) or (t == 0 and e[2] < 0) or (t == 1 and e[2] > 0)
+        return 2 if (t == 0 and e[2] < 0) or (t == 1 and e[2] > 0) else 1 if e[1] else 0
 
     def bonds(s, p, dirs, first, onto, x_inside=None, part=None):
         for t in range(2):
@@ -316,10 +324,10 @@
 
     def near_bonds(s, first, part):
         for p in (0, 1, 6, 7):
-            bonds(s, p, inner[p], first, part, part=part)
+            bonds(s, p, inner[p], first, part > 0, part=part)
 
         def middle(p, carry):
-            bonds(s, p, DIRS, first, part, part=part)
+            bonds(s, p, DIRS, first, part > 0, part=part)
             return carry
 
         lax.fori_loop(2, 6, middle, 0)
@@ -340,18 +348,23 @@
 
     def send(s, nc):
         pack_corners(s, nc)
-        start(s, nc, lambda d: d[2] == 0 and d[0])
+        start(s, nc, lambda d: d[0] and d[1] and not d[2])
         pack_columns(s, (0, 1, 6, 7), nc, False)
-        start(s, nc, lambda d: d[2] == 1)
+        start(s, nc, lambda d: d[0] and d[2])
+        start(s, nc, lambda d: not d[0] and d[2])
+        start(s, nc, lambda d: d[0] and not d[1] and not d[2])
         pack_rows(s, (0, 1, 6, 7), nc)
-        start(s, nc, lambda d: d[2] == 0 and not d[0])
+        start(s, nc, lambda d: not d[0] and not d[2])
 
     def run(s, nc, first, weight, go_on):
         turn_own(s, range(8), nc, False)
-        near_bonds(s, first, False)
-        wait_near(s, nc)
+        near_bonds(s, first, 0)
+        wait_beside(s, nc)
+        close_seam(s, range(8), nc, (1, 2))
+        near_bonds(s, first, 1)
+        wait_rows(s, nc)
         spread_near(s, nc)
-        near_bonds(s, first, True)
+        near_bonds(s, first, 2)
         advance(s, range(2, 6), weight)
         wait_sent(s, nc)
         go_on(lambda: (pack_columns(1 - s, range(2, 6), 3, True), pack_rows(1 - s, range(2, 6), 3)))
@@ -361,6 +374,8 @@
         advance(s, (0, 1, 6, 7), weight)
         go_on(lambda: send(1 - s, 3))
 
+    loads[4].wait()
+    loads[5].wait()
     loads[0].wait()
     for p in range(8):
         kind = cls[p]
@@ -384,6 +399,11 @@
 
     run(0, 5, True, HALF, lambda f: f())
 
+    stores = [
+        pltpu.make_async_copy(grid.at[STEPS % 2, 0:3, 2:10, 8:24], u_out, local_sem.at[1]),
+        pltpu.make_async_copy(speed, v_out, local_sem.at[2]),
+    ]
+
     def step(k, carry):
         weight = jnp.where(k == STEPS, HALF, DT)
 
@@ -392,17 +412,16 @@
             def _():
                 f()
 
+        @pl.when(k == STEPS)
+        def _():
+            stores[0].start()
+
         run(lax.rem(k, 2), 3, False, weight, go_on)
         return carry
 
     lax.fori_loop(1, STEPS + 1, step, 0)
 
-    stores = [
-        pltpu.make_async_copy(grid.at[STEPS % 2, 0:3, 2:10, 8:24], u_out, local_sem.at[1]),
-        pltpu.make_async_copy(speed, v_out, local_sem.at[2]),
-    ]
-    for c in stores:
-        c.start()
+    stores[1].start()
     for c in stores:
         c.wait()
 
@@ -411,13 +430,15 @@
     block = displacement.shape
     f32 = jnp.float32
     anywhere = pl.BlockSpec(memory_space=pl.ANY)
-    scalars = pl.BlockSpec(memory_space=pltpu.SMEM)
+    outside = pl.BlockSpec(memory_space=pltpu.HBM)
     return pl.pallas_call(
         kernel,
         out_shape=[jax.ShapeDtypeStruct(block, f32)] * 2,
-        in_specs=[scalars, scalars] + [anywhere] * 4,
+        in_specs=[outside] * 6,
         out_specs=[anywhere] * 2,
         scratch_shapes=[
+            pltpu.SMEM((4,), f32),
+            pltpu.SMEM((4,), f32),
             pltpu.VMEM((2, 5, 12, 32, 128), f32),
             pltpu.VMEM((4, 5, 12, 32, 128), f32),
             pltpu.VMEM((3, 8, 16, 128), f32),
@@ -432,12 +453,12 @@
             pltpu.VMEM((2, 4, 8, 128), f32),
             pltpu.VMEM((16, 128), f32),
             pltpu.VMEM((2, 3, 32, 128), f32),
-            pltpu.SemaphoreType.DMA((4,)),
+            pltpu.SemaphoreType.DMA((6,)),
             pltpu.SemaphoreType.DMA((NP,)),
             pltpu.SemaphoreType.DMA((2, NP)),
         ],
-        compiler_params=pltpu.CompilerParams(collective_id=0, has_side_effects=True),
-    )(stiffness, softening, displacement, velocity, classes, clamped)
+        compiler_params=pltpu.CompilerParams(collective_id=0, has_side_effects=True, vmem_limit_bytes=15 << 20),
+    )(*(pltpu.with_memory_space_constraint(x, pltpu.HBM) for x in (stiffness, softening, displacement, velocity, classes, clamped)))
 
 
 def solution(mesh):

time: 41.3 us -> 36.9 us (0.89)
  Pallas kernels: 38.2 us -> 34.8 us
  local copies, waits for them, and re-layouts: 2.34 us -> 1.36 us
    pallas_call x1, Pallas kernels: 38.2 us -> 34.8 us  [local(): pl.pallas_call(kernel, out_shape=[jax.ShapeDtypeStruct(block, f32)] * 2,...]
    unnamed x4 -> x2, local copies, waits for them, and re-layouts: 2.34 us -> 1.36 us
where the time goes in v3:
time: 36.9 us; the launch traced here: 36.8 us
  Pallas kernels  34.8 us (94%)
  local copies, waits for them, and re-layouts  1.36 us (4%)
  between operations  0.64 us (2%)
    pallas_call x1, Pallas kernels, local(): pl.pallas_call(kernel, out_shape=[jax.ShapeDtypeStruct(block, f32)] * 2,...  34.8 us
    unnamed x2, local copies, waits for them, and re-layouts  1.36 us

profile of v3, /device:TPU:121, one launch (start us, length us, event | category | flops | bytes accessed | tf_op | source)
XLA Modules:
  0.0 36.8 jit_solution(3391081859573441319)
XLA Ops:
  0.6 34.8 %shard_map.77 = (f32[3,8,16,128]{3,2,1,0:T(8,128)S(1)}, f32[3,8,16,128]{3,2,1,0:T(8,128)S(1)}) custom-call(f32[4]{0:T(128)} %table_c_in.1, f32[4]{0:T(128)} %table_q_in.1, f32[3,8,16,128]{3,2,1,0:T(8,128)} %u_in.1, f32[3,8,16,128]{3,2,1,0:T(8,128)} %v_in.1, s32[8,16,128]{2,1,0:T(8,128)} %class_in.1, s32[8,16,128]{2,1,0:T(8,128)} %clamp_in.1), custom_call_target="tpu_custom_call" | custom-call | tf_op jit(solution)/shard_map/pallas_call | solution.py:434
  35.4 0.7 %copy.10 = f32[3,8,16,128]{3,2,1,0:T(8,128)} copy(f32[3,8,16,128]{3,2,1,0:T(8,128)S(1)} %get-tuple-element.4) | data formatting | bytes 393216
  36.1 0.7 %copy.11 = f32[3,8,16,128]{3,2,1,0:T(8,128)} copy(f32[3,8,16,128]{3,2,1,0:T(8,128)S(1)} %get-tuple-element.5) | data formatting | bytes 393216

commit v4 on v3

--- a/solution.py
+++ b/solution.py
@@ -60,17 +60,6 @@
         beside()
         pl.when(has_right)(right)
 
-    zero = jnp.zeros((8, 128), jnp.float32)
-    for par in range(2):
-        for r in range(4):
-            rows = slice(8 * r, 8 * r + 8)
-            for c in range(5):
-                for plane in (0, 1, 10, 11):
-                    grid[par, c, plane, rows, :] = zero
-            qrecv[par, 0, rows, :] = zero
-            qrecv[par, 2, rows, :] = zero
-            crecv[par, r] = zero
-
     barrier = pltpu.get_barrier_semaphore()
 
     def greet(dx):
@@ -82,6 +71,25 @@
         return go
 
     by_side(greet(-1), greet(0), greet(1))
+
+    zero = jnp.zeros((8, 128), jnp.float32)
+
+    def clear(planes, slot, corners):
+        def go():
+            for par in range(2):
+                for r in range(4):
+                    rows = slice(8 * r, 8 * r + 8)
+                    for c in range(5):
+                        for plane in planes:
+                            grid[par, c, plane, rows, :] = zero
+                    qrecv[par, slot, rows, :] = zero
+                for q in corners:
+                    crecv[par, q] = zero
+
+        return go
+
+    pl.when(jnp.logical_not(has_left))(clear((0, 1), 0, (0, 1)))
+    pl.when(jnp.logical_not(has_right))(clear((10, 11), 2, (2, 3)))
 
     loads = [
         pltpu.make_async_copy(class_in, cls, local_sem.at[0]),
@@ -167,9 +175,9 @@
     def wait_rows(s, nc):
         each(s, nc, lambda d: d[0] == 0 and d[1], lambda t: t.wait_recv())
 
-    def wait_far(s, nc):
-        pl.when(has_left)(lambda: each(s, nc, lambda d: d[0] == 1, lambda t: t.wait_recv()))
-        pl.when(has_right)(lambda: each(s, nc, lambda d: d[0] == -1, lambda t: t.wait_recv()))
+    def wait_far(s, nc, which):
+        pl.when(has_left)(lambda: each(s, nc, lambda d: d[0] == 1 and which(d), lambda t: t.wait_recv()))
+        pl.when(has_right)(lambda: each(s, nc, lambda d: d[0] == -1 and which(d), lambda t: t.wait_recv()))
 
     def pack_corners(s, nc):
         for c in range(nc):
@@ -248,22 +256,25 @@
         turn_rows(s, range(8), nc)
         close_seam(s, range(8), nc, (0, 3))
 
+    def spread_planes(s, nc):
+        turn_own(s, (-1, 8), nc, True)
+        close_seam(s, (-1, 8), nc, (1, 2))
+
     def spread_far(s, nc):
         for c in range(nc):
             grid[s, c, 1, 7:8, :] = crecv[s, 0, c : c + 1, :]
             grid[s, c, 1, 24:25, :] = crecv[s, 1, c : c + 1, :]
             grid[s, c, 10, 7:8, :] = crecv[s, 2, c : c + 1, :]
             grid[s, c, 10, 24:25, :] = crecv[s, 3, c : c + 1, :]
-        turn_own(s, (-1, 8), nc, True)
         turn_rows(s, (-1, 8), nc)
-        close_seam(s, (-1, 8), nc)
+        close_seam(s, (-1, 8), nc, (0, 3))
 
     def needs_near(e, t):
         return 2 if (t == 0 and e[2] < 0) or (t == 1 and e[2] > 0) else 1 if e[1] else 0
 
-    def bonds(s, p, dirs, first, onto, x_inside=None, part=None):
+    def bonds(s, p, dirs, first, onto, part, x_inside=None):
         for t in range(2):
-            chosen = [e for e in dirs if part is None or needs_near(e, t) == part]
+            chosen = [e for e in dirs if needs_near(e, t) in part]
             mine = slice(8 * t, 8 * t + 8)
             base = slice(8 + 8 * t, 16 + 8 * t)
             centre = [grid[s, c, p + 2, base, :] for c in range(3)]
@@ -324,20 +335,20 @@
 
     def near_bonds(s, first, part):
         for p in (0, 1, 6, 7):
-            bonds(s, p, inner[p], first, part > 0, part=part)
+            bonds(s, p, inner[p], first, part > 0, (part,))
 
         def middle(p, carry):
-            bonds(s, p, DIRS, first, part > 0, part=part)
+            bonds(s, p, DIRS, first, part > 0, (part,))
             return carry
 
         lax.fori_loop(2, 6, middle, 0)
 
-    def far_bonds(s, first):
-        for p in (0, 1, 6, 7):
+    def far_bonds(s, planes, first, part):
+        for p in planes:
             inside = None
             if first:
-                inside = jnp.where(gx > 0, 1.0, 0.0) if p < 2 else jnp.where(gx < nx - 1, 1.0, 0.0)
-            bonds(s, p, [e for e in DIRS if e not in inner[p]], first, True, inside)
+                inside = jnp.where(has_left if p < 2 else has_right, 1.0, 0.0)
+            bonds(s, p, [e for e in DIRS if e not in inner[p]], first, True, part, inside)
 
     def advance(s, planes, weight):
         for p in planes:
@@ -346,14 +357,14 @@
                 speed[c, p] = new
                 grid[1 - s, c, p + 2, 8:24, :] = grid[s, c, p + 2, 8:24, :] + DT * new
 
-    def send(s, nc):
+    def send(s, nc, late):
         pack_corners(s, nc)
         start(s, nc, lambda d: d[0] and d[1] and not d[2])
-        pack_columns(s, (0, 1, 6, 7), nc, False)
+        pack_columns(s, late, nc, False)
         start(s, nc, lambda d: d[0] and d[2])
         start(s, nc, lambda d: not d[0] and d[2])
         start(s, nc, lambda d: d[0] and not d[1] and not d[2])
-        pack_rows(s, (0, 1, 6, 7), nc)
+        pack_rows(s, late, nc)
         start(s, nc, lambda d: not d[0] and not d[2])
 
     def run(s, nc, first, weight, go_on):
@@ -367,12 +378,19 @@
         near_bonds(s, first, 2)
         advance(s, range(2, 6), weight)
         wait_sent(s, nc)
-        go_on(lambda: (pack_columns(1 - s, range(2, 6), 3, True), pack_rows(1 - s, range(2, 6), 3)))
-        wait_far(s, nc)
+        pack_columns(1 - s, range(2, 6), 3, True)
+        pack_rows(1 - s, range(2, 6), 3)
+        wait_far(s, nc, lambda d: not d[1])
+        spread_planes(s, nc)
+        far_bonds(s, (1, 6, 0, 7), first, (0, 1))
+        advance(s, (1, 6), weight)
+        pack_columns(1 - s, (1, 6), 3, False)
+        pack_rows(1 - s, (1, 6), 3)
+        wait_far(s, nc, lambda d: d[1])
         spread_far(s, nc)
-        far_bonds(s, first)
-        advance(s, (0, 1, 6, 7), weight)
-        go_on(lambda: send(1 - s, 3))
+        far_bonds(s, (0, 7), first, (2,))
+        advance(s, (0, 7), weight)
+        go_on(lambda: send(1 - s, 3, (0, 7)))
 
     loads[4].wait()
     loads[5].wait()
@@ -391,7 +409,7 @@
     pack_columns(0, range(2, 6), 5, True)
     pack_rows(0, range(2, 6), 5)
     pl.semaphore_wait(barrier, 5 + jnp.where(has_left, 6, 0) + jnp.where(has_right, 6, 0))
-    send(0, 5)
+    send(0, 5, (0, 1, 6, 7))
     loads[2].wait()
     loads[3].wait()
     for p in range(8):
@@ -423,6 +441,17 @@
 
     stores[1].start()
     for c in stores:
+        c.wait()
+
+
+def put_out(u_from, v_from, u_to, v_to, sems):
+    moves = [
+        pltpu.make_async_copy(u_from, u_to, sems.at[0]),
+        pltpu.make_async_copy(v_from, v_to, sems.at[1]),
+    ]
+    for c in moves:
+        c.start()
+    for c in moves:
         c.wait()
 
 
@@ -431,7 +460,7 @@
     f32 = jnp.float32
     anywhere = pl.BlockSpec(memory_space=pl.ANY)
     outside = pl.BlockSpec(memory_space=pltpu.HBM)
-    return pl.pallas_call(
+    results = pl.pallas_call(
         kernel,
         out_shape=[jax.ShapeDtypeStruct(block, f32)] * 2,
         in_specs=[outside] * 6,
@@ -459,6 +488,14 @@
         ],
         compiler_params=pltpu.CompilerParams(collective_id=0, has_side_effects=True, vmem_limit_bytes=15 << 20),
     )(*(pltpu.with_memory_space_constraint(x, pltpu.HBM) for x in (stiffness, softening, displacement, velocity, classes, clamped)))
+    return pl.pallas_call(
+        put_out,
+        out_shape=[jax.ShapeDtypeStruct(block, f32)] * 2,
+        in_specs=[anywhere] * 2,
+        out_specs=[anywhere] * 2,
+        scratch_shapes=[pltpu.SemaphoreType.DMA((2,))],
+        compiler_params=pltpu.CompilerParams(vmem_limit_bytes=1 << 20),
+    )(*results)
 
 
 def solution(mesh):

time: 36.9 us -> 36.1 us (0.978)
  local copies, waits for them, and re-layouts: 1.36 us -> 0 us
  Pallas kernels: 34.8 us -> 35.3 us
    unnamed x2 -> x0, local copies, waits for them, and re-layouts: 1.36 us -> none
    pallas_call x0 -> x1, Pallas kernels: none -> 0.76 us  [local(): pl.pallas_call(put_out, out_shape=[jax.ShapeDtypeStruct(block, f32)] * 2,...]
where the time goes in v4:
time: 36.1 us; the launch traced here: 36 us
  Pallas kernels  35.3 us (98%)
  between operations  0.64 us (2%)
    pallas_call x1, Pallas kernels, local(): pl.pallas_call(kernel, out_shape=[jax.ShapeDtypeStruct(block, f32)] * 2,...  34.6 us
    pallas_call x1, Pallas kernels, local(): pl.pallas_call(put_out, out_shape=[jax.ShapeDtypeStruct(block, f32)] * 2,...  0.76 us

profile of v4, /device:TPU:121, one launch (start us, length us, event | category | flops | bytes accessed | tf_op | source)
XLA Modules:
  0.0 36.0 jit_solution(5717993141779966062)
XLA Ops:
  0.6 34.6 %shard_map.77 = (f32[3,8,16,128]{3,2,1,0:T(8,128)S(1)}, f32[3,8,16,128]{3,2,1,0:T(8,128)S(1)}) custom-call(f32[4]{0:T(128)} %table_c_in.1, f32[4]{0:T(128)} %table_q_in.1, f32[3,8,16,128]{3,2,1,0:T(8,128)} %u_in.1, f32[3,8,16,128]{3,2,1,0:T(8,128)} %v_in.1, s32[8,16,128]{2,1,0:T(8,128)} %class_in.1, s32[8,16,128]{2,1,0:T(8,128)} %clamp_in.1), custom_call_target="tpu_custom_call" | custom-call | tf_op jit(solution)/shard_map/pallas_call | solution.py:463
  35.2 0.8 %shard_map.78 = (f32[3,8,16,128]{3,2,1,0:T(8,128)}, f32[3,8,16,128]{3,2,1,0:T(8,128)}) custom-call(f32[3,8,16,128]{3,2,1,0:T(8,128)S(1)} %get-tuple-element.4.u_from, f32[3,8,16,128]{3,2,1,0:T(8,128)S(1)} %get-tuple-element.5.v_from), custom_call_target="tpu_custom_call" | custom-call | tf_op jit(solution)/shard_map/pallas_call | solution.py:491

commit v5 on v4

--- a/solution.py
+++ b/solution.py
@@ -38,8 +38,8 @@
 
 def kernel(
     table_c_in, table_q_in, u_in, v_in, class_in, clamp_in,
-    u_out, v_out,
-    table_c, table_q, grid, turned, speed, cls, clm, free, acc, coef,
+    u_out, speed,
+    table_c, table_q, grid, turned, cls, clm, free, acc, coef,
     zsend, zrecv, csend, crecv, qsend, qrecv,
     local_sem, send_sem, recv_sem,
 ):
@@ -419,7 +419,6 @@
 
     stores = [
         pltpu.make_async_copy(grid.at[STEPS % 2, 0:3, 2:10, 8:24], u_out, local_sem.at[1]),
-        pltpu.make_async_copy(speed, v_out, local_sem.at[2]),
     ]
 
     def step(k, carry):
@@ -439,7 +438,6 @@
 
     lax.fori_loop(1, STEPS + 1, step, 0)
 
-    stores[1].start()
     for c in stores:
         c.wait()
 
@@ -464,13 +462,12 @@
         kernel,
         out_shape=[jax.ShapeDtypeStruct(block, f32)] * 2,
         in_specs=[outside] * 6,
-        out_specs=[anywhere] * 2,
+        out_specs=[anywhere, pl.BlockSpec(memory_space=pltpu.VMEM)],
         scratch_shapes=[
             pltpu.SMEM((4,), f32),
             pltpu.SMEM((4,), f32),
             pltpu.VMEM((2, 5, 12, 32, 128), f32),
             pltpu.VMEM((4, 5, 12, 32, 128), f32),
-            pltpu.VMEM((3, 8, 16, 128), f32),
             pltpu.VMEM((8, 16, 128), jnp.int32),
             pltpu.VMEM((8, 16, 128), jnp.int32),
             pltpu.VMEM((8, 16, 128), f32),

time: 36.1 us -> 35.8 us (level)
  no operation moved by 1% of the time
where the time goes in v5:
time: 35.8 us; the launch traced here: 35.7 us
  Pallas kernels  35 us (98%)
  between operations  0.64 us (2%)
    pallas_call x1, Pallas kernels, local(): pl.pallas_call(kernel, out_shape=[jax.ShapeDtypeStruct(block, f32)] * 2,...  34.3 us
    pallas_call x1, Pallas kernels, local(): pl.pallas_call(put_out, out_shape=[jax.ShapeDtypeStruct(block, f32)] * 2,...  0.76 us

profile of v5, /device:TPU:121, one launch (start us, length us, event | category | flops | bytes accessed | tf_op | source)
XLA Modules:
  0.0 35.7 jit_solution(8896417024988698740)
XLA Ops:
  0.6 34.3 %shard_map.77 = (f32[3,8,16,128]{3,2,1,0:T(8,128)S(1)}, f32[3,8,16,128]{3,2,1,0:T(8,128)S(1)}) custom-call(f32[4]{0:T(128)} %table_c_in.1, f32[4]{0:T(128)} %table_q_in.1, f32[3,8,16,128]{3,2,1,0:T(8,128)} %u_in.1, f32[3,8,16,128]{3,2,1,0:T(8,128)} %v_in.1, s32[8,16,128]{2,1,0:T(8,128)} %class_in.1, s32[8,16,128]{2,1,0:T(8,128)} %clamp_in.1), custom_call_target="tpu_custom_call" | custom-call | tf_op jit(solution)/shard_map/pallas_call | solution.py:461
  34.9 0.8 %shard_map.78 = (f32[3,8,16,128]{3,2,1,0:T(8,128)}, f32[3,8,16,128]{3,2,1,0:T(8,128)}) custom-call(f32[3,8,16,128]{3,2,1,0:T(8,128)S(1)} %get-tuple-element.4.u_from, f32[3,8,16,128]{3,2,1,0:T(8,128)S(1)} %get-tuple-element.5.v_from), custom_call_target="tpu_custom_call" | custom-call | tf_op jit(solution)/shard_map/pallas_call | solution.py:488
